TPU v7x, 128 devices: a whole 4x4x4 slice. The times are simulated.
128 devices in a mesh: ctx: 32 (over x, z, y_lo), fsdp: 4 (over y_hi, core).
Axes of the slice: x: 4, y: 4 (y_hi: 2, y_lo: 2; y = y_hi * 2 + y_lo), z: 4, core: 2. Of those that a mesh axis runs over, the one named last changes fastest.
Arguments:
- x_cur: bfloat16 [4, 8192, 2048], P('fsdp', 'ctx'), may hold values from -6 to 6
- x_next: bfloat16 [4, 8192, 2048], P('fsdp', 'ctx'), may hold values from -6 to 6
- cot_cur: bfloat16 [4, 8192, 2048], P('fsdp', 'ctx'), may hold values from -6 to 6
- cot_next: bfloat16 [4, 8192, 2048], P('fsdp', 'ctx'), may hold values from -6 to 6
- w_q: bfloat16 [2048, 1024], P('fsdp')
- w_kv: bfloat16 [2048, 512], P('fsdp')
- w_out: bfloat16 [2048, 1024], P('fsdp'), may hold values from -0.1875 to 0.1875
Outputs:
- x_prev: bfloat16 [4, 8192, 2048], P('fsdp', 'ctx')
- grad_cur: bfloat16 [4, 8192, 2048], P('fsdp', 'ctx')
- grad_weights: float32 [2048, 2560], P(('ctx', 'fsdp'))
All inputs are finite; a program needn't handle non-finite values.
Results may differ from a plain program's by a relative error of at most 0.015.
The roundings to bfloat16 on the way count: a program that leaves them out, or rounds other values in their place, can miss the bound.
Values may be sent and summed in bfloat16 or wider, within the bound.
No kernel may reach another device: no remote copies, remote signals or barrier semaphores. Data moves between devices by JAX's collectives and lax.ppermute only.
A program may use at most 192 MiB of HBM per device.

v0:
```python
import math

import jax
import jax.numpy as jnp
from jax import lax
from jax.sharding import PartitionSpec as P

QUERY_HEADS = 8
KEY_VALUE_HEADS = 2
HEAD_SIZE = 128
WINDOW_TOKENS = 1024


EPS = 1e-05


def from_behind(value, axis, steps):
    count = lax.axis_size(axis)
    leading, last = (max(0, -steps), min(count, count - steps))
    return lax.ppermute(value, axis, [(source, source + steps) for source in range(leading, last)])


def normalize(rows):
    values = rows.astype(jnp.float32)
    inv_rms = lax.rsqrt(jnp.mean(values * values, axis=-1, keepdims=True) + EPS)
    return (values * inv_rms, inv_rms)


def head_block(items, allowed):
    quer3, keys2, vals2, grad3 = items
    scale = 1.0 / math.sqrt(HEAD_SIZE)
    scores = jnp.einsum("imd,jd->mij", quer3, keys2, preferred_element_type=jnp.float32) * scale
    scores = jnp.where(allowed[None], scores, -jnp.inf)
    top = jnp.max(scores, axis=-1, keepdims=True)
    expo = jnp.exp(scores - top)
    probs = expo / jnp.sum(expo, axis=-1, keepdims=True)
    probs_low = probs.astype(jnp.bfloat16)
    attended = jnp.einsum("mij,jd->imd", probs_low, vals2, preferred_element_type=jnp.float32)
    grad_probs = jnp.einsum("imd,jd->mij", grad3, vals2, preferred_element_type=jnp.float32)
    delta = jnp.einsum("imd,imd->mi", grad3.astype(jnp.float32), attended)
    grad_scores = (probs * (grad_probs - delta[..., None]) * scale).astype(jnp.bfloat16)
    grad_query = jnp.einsum("mij,jd->imd", grad_scores, keys2, preferred_element_type=jnp.float32)
    key_gradient = jnp.einsum("mij,imd->jd", grad_scores, quer3, preferred_element_type=jnp.float32)
    value_gradient = jnp.einsum("mij,imd->jd", probs_low, grad3, preferred_element_type=jnp.float32)
    return (
        attended.astype(jnp.bfloat16),
        grad_query.astype(jnp.bfloat16),
        key_gradient.astype(jnp.bfloat16),
        value_gradient.astype(jnp.bfloat16),
    )


def window_block(query_rows, key_value_pairs, output_gradient, base):
    window_extent = key_value_pairs.shape[0]
    element_count = query_rows.shape[0]
    query_group = QUERY_HEADS // KEY_VALUE_HEADS
    query_pos = base + jnp.arange(element_count, dtype=jnp.int32)
    key_pos = base - WINDOW_TOKENS + jnp.arange(window_extent, dtype=jnp.int32)
    offset = query_pos[:, None] - key_pos[None, :]
    allowed = (offset >= 0) & (offset < WINDOW_TOKENS) & (key_pos[None, :] >= 0)
    query_grouped = query_rows.reshape(
        element_count, KEY_VALUE_HEADS, query_group, HEAD_SIZE
    ).transpose(1, 0, 2, 3)
    gradient_grouped = output_gradient.reshape(
        element_count, KEY_VALUE_HEADS, query_group, HEAD_SIZE
    ).transpose(1, 0, 2, 3)
    key_tensor = (
        key_value_pairs[:, : KEY_VALUE_HEADS * HEAD_SIZE]
        .reshape(window_extent, KEY_VALUE_HEADS, HEAD_SIZE)
        .transpose(1, 0, 2)
    )
    value_tensor = (
        key_value_pairs[:, KEY_VALUE_HEADS * HEAD_SIZE :]
        .reshape(window_extent, KEY_VALUE_HEADS, HEAD_SIZE)
        .transpose(1, 0, 2)
    )

    def per_head(items):
        return head_block(items, allowed)

    attended, grad_query, key_gradient, value_gradient = lax.map(
        per_head, (query_grouped, key_tensor, value_tensor, gradient_grouped)
    )
    attended = attended.transpose(1, 0, 2, 3).reshape(element_count, QUERY_HEADS * HEAD_SIZE)
    grad_query = grad_query.transpose(1, 0, 2, 3).reshape(element_count, QUERY_HEADS * HEAD_SIZE)
    key_gradient = key_gradient.transpose(1, 0, 2).reshape(
        window_extent, KEY_VALUE_HEADS * HEAD_SIZE
    )
    value_gradient = value_gradient.transpose(1, 0, 2).reshape(
        window_extent, KEY_VALUE_HEADS * HEAD_SIZE
    )
    value_partial_sum = jnp.concatenate([key_gradient, value_gradient], 1)
    return (attended, grad_query, value_partial_sum)


def shards(x_cur, x_next, cot_cur, cot_next, w_q, w_kv, w_out):
    full_q, full_kv, full_out = (
        lax.all_gather(w_q, "fsdp", axis=0, tiled=True),
        lax.all_gather(w_kv, "fsdp", axis=0, tiled=True),
        lax.all_gather(w_out, "fsdp", axis=0, tiled=True),
    )
    seq_count, shard, width = x_cur.shape
    base = lax.axis_index("ctx") * shard
    preds = WINDOW_TOKENS // shard
    normed, inv_rms = normalize(x_cur)
    hidden = normed.astype(jnp.bfloat16)
    query_rows = jnp.einsum(
        "sid,dc->sic", hidden, full_q, preferred_element_type=jnp.float32
    ).astype(jnp.bfloat16)
    key_value_pairs = jnp.einsum(
        "sid,dc->sic", hidden, full_kv, preferred_element_type=jnp.float32
    ).astype(jnp.bfloat16)
    grad_attn = (
        2.0 * jnp.einsum("sid,dc->sic", cot_next, full_out, preferred_element_type=jnp.float32)
    ).astype(jnp.bfloat16)
    earlier = []
    for hop in range(1, preds + 1):
        earlier.append(from_behind(key_value_pairs, "ctx", hop))
    window_keys = jnp.concatenate(earlier[::-1] + [key_value_pairs], axis=1)

    def per_sequence(items):
        q_rows, kv_rows, g_rows = items
        return window_block(q_rows, kv_rows, g_rows, base)

    attended, grad_query, value_partial_sum = lax.map(
        per_sequence, (query_rows, window_keys, grad_attn)
    )
    owned = value_partial_sum[:, WINDOW_TOKENS:].astype(jnp.float32)
    for hop in range(1, preds + 1):
        piece = value_partial_sum[
            :, WINDOW_TOKENS - hop * shard : WINDOW_TOKENS - (hop - 1) * shard
        ]
        owned = owned + from_behind(piece, "ctx", -hop).astype(jnp.float32)
    grad_kv = owned.astype(jnp.bfloat16)
    layer_out = jnp.einsum("sic,dc->sid", attended, full_out, preferred_element_type=jnp.float32)
    x_prev = (x_next.astype(jnp.float32) - 2.0 * layer_out).astype(jnp.bfloat16)
    grad_hidden = jnp.einsum("sic,dc->sid", grad_query, full_q, preferred_element_type=jnp.float32)
    grad_hidden = grad_hidden + jnp.einsum(
        "sic,dc->sid", grad_kv, full_kv, preferred_element_type=jnp.float32
    )
    grad_x = inv_rms * (
        grad_hidden - normed * jnp.mean(grad_hidden * normed, axis=-1, keepdims=True)
    )
    grad_cur = (cot_cur.astype(jnp.float32) + grad_x).astype(jnp.bfloat16)
    hidden_rows = hidden.reshape(seq_count * shard, width)
    cot_rows = cot_next.reshape(seq_count * shard, width)
    left_rows = jnp.concatenate([grad_query, grad_kv], axis=2).reshape(seq_count * shard, -1)
    attended_rows = attended.reshape(seq_count * shard, -1)
    contract_rows = (((0,), (0,)), ((), ()))
    ctx_count = lax.axis_size("ctx")
    fsdp_count = lax.axis_size("fsdp")
    term_in = lax.dot_general(
        hidden_rows, left_rows, contract_rows, preferred_element_type=jnp.float32
    )
    term_out = 2.0 * lax.dot_general(
        cot_rows, attended_rows, contract_rows, preferred_element_type=jnp.float32
    )
    summed = lax.psum_scatter(
        jnp.concatenate([term_in, term_out], axis=1),
        ("ctx", "fsdp"),
        scatter_dimension=0,
        tiled=True,
    )
    token_total = seq_count * shard * ctx_count * fsdp_count
    grad_weights = summed * (1.0 / math.sqrt(token_total))
    return (x_prev, grad_cur, grad_weights)


def solution(mesh):
    in_specs = (
        P("fsdp", "ctx", None),
        P("fsdp", "ctx", None),
        P("fsdp", "ctx", None),
        P("fsdp", "ctx", None),
        P("fsdp", None),
        P("fsdp", None),
        P("fsdp", None),
    )
    out_specs = (P("fsdp", "ctx", None), P("fsdp", "ctx", None), P(("ctx", "fsdp"), None))
    return jax.shard_map(shards, mesh=mesh, in_specs=in_specs, out_specs=out_specs, check_vma=False)
```

profile of v0, /device:TPU:0, one launch (start us, length us, event | category | flops | bytes accessed | tf_op | source)
XLA Modules:
  0.0 945.0 jit_solution(4321865399467720031)
XLA Ops:
  9.8 29.0 %all-gather.4.cloned.1.call-done = bf16[2048,512]{1,0:T(8,128)(2,1)} async-done(((bf16[512,512]{1,0:T(8,128)(2,1)}), bf16[2048,512]{1,0:T(8,128)(2,1)}) %all-gather.4.cloned.1.call-update) | async-done | bytes 2097168 | tf_op jit(solution)/shard_map/all_gather | solution.py:99
  38.8 2.3 fusion.71
  41.1 5.1 collective-permute-start
  46.2 2.6 collective-permute-start.1
  48.9 2.5 collective-permute-start.2
  51.4 4.9 collective-permute-start.3
  56.4 3.8 collective-permute-done.1
  60.3 6.2 collective-permute-done.2
  66.5 4.0 collective-permute-done.3
  72.7 14.0 %all-gather.6.cloned.1.call-done = bf16[2048,1024]{1,0:T(8,128)(2,1)} async-done(((bf16[512,1024]{1,0:T(8,128)(2,1)}), bf16[2048,1024]{1,0:T(8,128)(2,1)}) %all-gather.6.cloned.1.call-update) | async-done | bytes 4194320 | tf_op jit(solution)/shard_map/all_gather | solution.py:98
  86.7 3.5 convolution_convert_fusion.1
  90.6 37.8 %all-gather.8.cloned.1.call-done = bf16[2048,1024]{1,0:T(8,128)(2,1)} async-done(((bf16[512,1024]{1,0:T(8,128)(2,1)}), bf16[2048,1024]{1,0:T(8,128)(2,1)}) %all-gather.8.cloned.1.call-update) | async-done | bytes 4194320 | tf_op jit(solution)/shard_map/all_gather | solution.py:100
  128.4 4.2 fusion.70
  132.6 1.4 reshape.120
  134.0 1.2 copy_bitcast_fusion
  135.2 46.7 %while.29 = (s32[]{:T(128)}, bf16[2,256,4,128]{1,3,2,0:T(8,128)(2,1)}, bf16[2,256,4,128]{1,3,2,0:T(8,128)(2,1)}, bf16[2,1280,128]{1,2,0:T(8,128)(2,1)}, bf16[2,1...) while((s32[]{:T(128)}, ...), condition=%wide.region_4.5_spmd.clone, body=%wide.region_1.4_spmd.clone.sunk | while | flops 2030305536 | bytes 79461984 | solution.py:81
  137.3 5.2 exponential_reduce_fusion.2
  142.6 4.0 fusion.133
  146.6 1.9 fusion.138
  149.2 4.0 fusion.136
  153.4 2.7 fusion.139
  156.2 1.3 fusion.137
  160.7 5.2 exponential_reduce_fusion.2
  165.9 4.0 fusion.133
  169.9 1.9 fusion.138
  172.5 4.0 fusion.136
  176.8 2.7 fusion.139
  179.6 1.2 fusion.137
  181.9 1.4 maximum_bitcast_fusion
  183.4 1.3 collective-permute-start.4
  184.7 1.3 collective-permute-start.7
  186.0 1.3 collective-permute-start.6
  187.3 1.5 collective-permute-start.5
  188.8 1.3 multiply_bitcast_fusion
  190.0 3.7 collective-permute-done.4
  193.7 3.5 collective-permute-done.7
  197.3 7.3 collective-permute-done.6
  204.5 5.0 collective-permute-done.5
  209.7 2.9 fusion.75
  212.6 11.0 %pad_maximum_fusion = f32[2048,2560]{0,1:T(8,128)} fusion(f32[2048,1024]{0,1:T(8,128)S(1)} %multiply_bitcast_fusion, f32[2048,1536]{0,1:T(8,128)S(1)} %fusion.75), kind=kLoop, calls=%fused_computation.63 | loop fusion | flops 5242880 | bytes 41943040 | tf_op jit(solution)/shard_map/concatenate | solution.py:159
  223.6 20.0 %copy.54 = f32[2048,2560]{1,0:T(8,128)} copy(f32[2048,2560]{0,1:T(8,128)} %pad_maximum_fusion) | data formatting | bytes 41943040
  243.7 3.8 fusion.88
  247.6 2.3 fusion.63
  251.1 1.6 fusion.68
  252.7 680.9 %reduce-scatter.4.cloned.1.call-done = f32[16,2560]{1,0:T(8,128)} async-done(((f32[2048,2560]{1,0:T(8,128)}), f32[16,2560]{1,0:T(8,128)}) %reduce-scatter.4.cloned.1.call-update) | async-done | bytes 163856
  933.6 1.3 copy.55
  934.9 1.2 broadcast_multiply_fusion
  936.1 2.4 copy.40
  (95 shorter events, 14.7 us)
Async XLA Ops:
  7.2 121.2 %copy-start = (bf16[1,256,2048]{2,1,0:T(8,128)(2,1)S(1)}, bf16[1,256,2048]{2,1,0:T(8,128)(2,1)}, u32[]{:S(2)}) copy-start(bf16[1,256,2048]{2,1,0:T(8,128)(2,1)} %param.12) | copy-start | bytes 3145732
  7.2 2.3 copy-start.2
  7.2 31.6 %all-gather.4.cloned.1.call-start = ((), (), s32[]{:S(2)}) async-start(), calls=%async_computation.1 | async-start | bytes 2621440 | tf_op jit(solution)/shard_map/all_gather | solution.py:99
  7.9 78.8 %all-gather.6.cloned.1.call-start = ((), (), s32[]{:S(2)}) async-start(), calls=%async_computation.2 | async-start | bytes 5242880 | tf_op jit(solution)/shard_map/all_gather | solution.py:98
  8.7 119.7 %all-gather.8.cloned.1.call-start = ((), (), s32[]{:S(2)}) async-start(), calls=%async_computation.3 | async-start | bytes 5242880 | tf_op jit(solution)/shard_map/all_gather | solution.py:100
  9.4 924.2 %reduce-scatter.4.cloned.1.call-start = ((), (), s32[]{:S(2)}) async-start(), calls=%async_computation.4 | async-start | bytes 21135360
  41.1 15.2 %collective-permute-start = (bf16[1,256,512]{2,1,0:T(8,128)(2,1)S(1)}, bf16[1,256,512]{2,1,0:T(8,128)(2,1)S(1)}, u32[]{:S(2)}, u32[]{:S(2)}) collective-permute-start(bf16[1,256,512]{2,1,0:T(8,128)(2,1)S(1)} %fusion.71), channel_id=1, source_target_pairs={{0,16},{4,20},{8,24},{12,28},{16,32},{20,36},{24,40},{28,44},{32,4... | collective-permute-start | bytes 786440 | tf_op jit(solution)/shard_map/ppermute | solution.py:20
  46.2 14.0 %collective-permute-start.1 = (bf16[1,256,512]{2,1,0:T(8,128)(2,1)S(1)}, bf16[1,256,512]{2,1,0:T(8,128)(2,1)S(1)}, u32[]{:S(2)}, u32[]{:S(2)}) collective-permute-start(bf16[1,256,512]{2,1,0:T(8,128)(2,1)S(1)} %fusion.71), channel_id=1, source_target_pairs={{0,12},{4,16},{8,20},{12,24},{16,28},{20,32},{24,36},{28,40},{32,4... | collective-permute-start | bytes 786440 | tf_op jit(solution)/shard_map/ppermute | solution.py:20
  48.9 17.6 %collective-permute-start.2 = (bf16[1,256,512]{2,1,0:T(8,128)(2,1)S(1)}, bf16[1,256,512]{2,1,0:T(8,128)(2,1)S(1)}, u32[]{:S(2)}, u32[]{:S(2)}) collective-permute-start(bf16[1,256,512]{2,1,0:T(8,128)(2,1)S(1)} %fusion.71), channel_id=1, source_target_pairs={{0,8},{4,12},{8,16},{12,20},{16,24},{20,28},{24,32},{28,36},{32,40... | collective-permute-start | bytes 786440 | tf_op jit(solution)/shard_map/ppermute | solution.py:20
  51.4 19.1 %collective-permute-start.3 = (bf16[1,256,512]{2,1,0:T(8,128)(2,1)S(1)}, bf16[1,256,512]{2,1,0:T(8,128)(2,1)S(1)}, u32[]{:S(2)}, u32[]{:S(2)}) collective-permute-start(bf16[1,256,512]{2,1,0:T(8,128)(2,1)S(1)} %fusion.71), channel_id=1, source_target_pairs={{0,4},{4,8},{8,12},{12,16},{16,20},{20,24},{24,28},{28,32},{32,36}... | collective-permute-start | bytes 786440 | tf_op jit(solution)/shard_map/ppermute | solution.py:20
  142.6 6.6 slice-start
  146.5 2.0 copy-start.4
  146.5 2.0 copy-start.7
  146.6 2.6 slice-start.1
  149.1 4.2 copy-start.8
  149.2 4.2 copy-start.10
  153.4 2.8 copy-start.1
  153.4 2.8 copy-start.3
  165.9 6.6 slice-start
  169.9 2.0 copy-start.4
  169.9 2.0 copy-start.7
  169.9 2.6 slice-start.1
  172.4 4.2 copy-start.8
  172.5 4.2 copy-start.10
  176.8 2.8 copy-start.1
  176.8 2.8 copy-start.3
  181.9 6.9 copy-start.9
  183.4 10.3 %collective-permute-start.4 = (bf16[1,256,512]{1,2,0:T(8,128)(2,1)S(1)}, bf16[1,256,512]{1,2,0:T(8,128)(2,1)S(1)}, u32[]{:S(2)}, u32[]{:S(2)}) collective-permute-start(bf16[1,256,512]{1,2,0:T(8,128)(2,1)S(1)} %get-tuple-element.154), channel_id=1, source_target_pairs={{4,0},{8,4},{12,8},{16,12},{20,16},{24,20},{28,24},{32,28},{36,32}... | collective-permute-start | bytes 786440 | tf_op jit(solution)/shard_map/ppermute | solution.py:20
  184.7 12.6 %collective-permute-start.7 = (bf16[1,256,512]{1,2,0:T(8,128)(2,1)S(1)}, bf16[1,256,512]{1,2,0:T(8,128)(2,1)S(1)}, u32[]{:S(2)}, u32[]{:S(2)}) collective-permute-start(bf16[1,256,512]{1,2,0:T(8,128)(2,1)S(1)} %get-tuple-element.155), channel_id=1, source_target_pairs={{16,0},{20,4},{24,8},{28,12},{32,16},{36,20},{40,24},{44,28},{48,3... | collective-permute-start | bytes 786440 | tf_op jit(solution)/shard_map/ppermute | solution.py:20
  186.0 18.6 %collective-permute-start.6 = (bf16[1,256,512]{1,2,0:T(8,128)(2,1)S(1)}, bf16[1,256,512]{1,2,0:T(8,128)(2,1)S(1)}, u32[]{:S(2)}, u32[]{:S(2)}) collective-permute-start(bf16[1,256,512]{1,2,0:T(8,128)(2,1)S(1)} %get-tuple-element.156), channel_id=1, source_target_pairs={{12,0},{16,4},{20,8},{24,12},{28,16},{32,20},{36,24},{40,28},{44,3... | collective-permute-start | bytes 786440 | tf_op jit(solution)/shard_map/ppermute | solution.py:20
  187.3 22.2 %collective-permute-start.5 = (bf16[1,256,512]{1,2,0:T(8,128)(2,1)S(1)}, bf16[1,256,512]{1,2,0:T(8,128)(2,1)S(1)}, u32[]{:S(2)}, u32[]{:S(2)}) collective-permute-start(bf16[1,256,512]{1,2,0:T(8,128)(2,1)S(1)} %get-tuple-element.157), channel_id=1, source_target_pairs={{8,0},{12,4},{16,8},{20,12},{24,16},{28,20},{32,24},{36,28},{40,32... | collective-permute-start | bytes 786440 | tf_op jit(solution)/shard_map/ppermute | solution.py:20
  243.7 3.8 copy-start.11
  243.7 3.9 copy-start.12
  247.6 2.3 copy-start.5
  249.8 1.2 copy-start.6
Sparse Core Ops, SparseCore 0:
  9.7 29.0 all-gather.3
  40.5 46.1 all-gather.5
  88.4 39.9 all-gather.7
  243.8 689.7 reduce-scatter.3
where the time goes:
time: 946 us; the launch traced here: 945 us
  waiting for transfers between devices  797 us (84%)
  matrix products  52.8 us (6%)
  local copies, waits for them, and re-layouts  32.1 us (3%)
  other arithmetic  27.7 us (3%)
  starting transfers between devices  20.6 us (2%)
  between operations  14.1 us (1%)
    unnamed x5, waiting for transfers between devices  683 us
    all_gather x1, waiting for transfers between devices, shards(): lax.all_gather(w_out, 'fsdp', axis=0, tiled=True)  37.8 us
    ppermute x8, waiting for transfers between devices, from_behind(): lax.ppermute(value, axis, [(source, source + steps) for source in range(l...  33.5 us
    all_gather x1, waiting for transfers between devices, shards(): lax.all_gather(w_kv, 'fsdp', axis=0, tiled=True)  29 us
    unnamed x22, local copies, waits for them, and re-layouts  24.2 us
    ppermute x8, starting transfers between devices, from_behind(): lax.ppermute(value, axis, [(source, source + steps) for source in range(l...  20.5 us
  transfers between devices with their start and end apart: 12, of which 11 were waited for; matrix products, arithmetic and copies ran while one was open for 2% of the time, Pallas kernels for 0%

commit v1 on v0

--- a/solution.py
+++ b/solution.py
@@ -3,6 +3,7 @@
 import jax
 import jax.numpy as jnp
 from jax import lax
+from jax.sharding import Mesh
 from jax.sharding import PartitionSpec as P
 
 QUERY_HEADS = 8
@@ -13,11 +14,19 @@
 
 EPS = 1e-05
 
+CTX = ("x", "z", "yl")
+FSDP = ("yh", "c")
+CHIPS = ("x", "z", "yl", "yh")
+
 
 def from_behind(value, axis, steps):
     count = lax.axis_size(axis)
     leading, last = (max(0, -steps), min(count, count - steps))
     return lax.ppermute(value, axis, [(source, source + steps) for source in range(leading, last)])
+
+
+def swap_cores(value):
+    return lax.ppermute(value, "c", [(0, 1), (1, 0)])
 
 
 def normalize(rows):
@@ -95,12 +104,12 @@
 
 def shards(x_cur, x_next, cot_cur, cot_next, w_q, w_kv, w_out):
     full_q, full_kv, full_out = (
-        lax.all_gather(w_q, "fsdp", axis=0, tiled=True),
-        lax.all_gather(w_kv, "fsdp", axis=0, tiled=True),
-        lax.all_gather(w_out, "fsdp", axis=0, tiled=True),
+        lax.all_gather(w_q, FSDP, axis=0, tiled=True),
+        lax.all_gather(w_kv, FSDP, axis=0, tiled=True),
+        lax.all_gather(w_out, FSDP, axis=0, tiled=True),
     )
     seq_count, shard, width = x_cur.shape
-    base = lax.axis_index("ctx") * shard
+    base = lax.axis_index(CTX) * shard
     preds = WINDOW_TOKENS // shard
     normed, inv_rms = normalize(x_cur)
     hidden = normed.astype(jnp.bfloat16)
@@ -115,7 +124,7 @@
     ).astype(jnp.bfloat16)
     earlier = []
     for hop in range(1, preds + 1):
-        earlier.append(from_behind(key_value_pairs, "ctx", hop))
+        earlier.append(from_behind(key_value_pairs, CTX, hop))
     window_keys = jnp.concatenate(earlier[::-1] + [key_value_pairs], axis=1)
 
     def per_sequence(items):
@@ -130,7 +139,7 @@
         piece = value_partial_sum[
             :, WINDOW_TOKENS - hop * shard : WINDOW_TOKENS - (hop - 1) * shard
         ]
-        owned = owned + from_behind(piece, "ctx", -hop).astype(jnp.float32)
+        owned = owned + from_behind(piece, CTX, -hop).astype(jnp.float32)
     grad_kv = owned.astype(jnp.bfloat16)
     layer_out = jnp.einsum("sic,dc->sid", attended, full_out, preferred_element_type=jnp.float32)
     x_prev = (x_next.astype(jnp.float32) - 2.0 * layer_out).astype(jnp.bfloat16)
@@ -142,39 +151,69 @@
         grad_hidden - normed * jnp.mean(grad_hidden * normed, axis=-1, keepdims=True)
     )
     grad_cur = (cot_cur.astype(jnp.float32) + grad_x).astype(jnp.bfloat16)
-    hidden_rows = hidden.reshape(seq_count * shard, width)
-    cot_rows = cot_next.reshape(seq_count * shard, width)
-    left_rows = jnp.concatenate([grad_query, grad_kv], axis=2).reshape(seq_count * shard, -1)
-    attended_rows = attended.reshape(seq_count * shard, -1)
+    core = lax.axis_index("c")
+    token_total = seq_count * shard * lax.axis_size(CTX) * lax.axis_size(FSDP)
+    rows_in = hidden.reshape(seq_count * shard, width)
+    rows_out = cot_next.reshape(seq_count * shard, width)
+    both_in = jnp.concatenate([rows_in, swap_cores(rows_in)], axis=0)
+    both_out = jnp.concatenate([rows_out, swap_cores(rows_out)], axis=0)
+
+    def halves(rows):
+        rows = rows.reshape(seq_count * shard, -1)
+        half = rows.shape[1] // 2
+        first = core == 0
+        return (
+            jnp.where(first, rows[:, :half], rows[:, half:]),
+            jnp.where(first, rows[:, half:], rows[:, :half]),
+        )
+
+    kept, sent = zip(halves(grad_query), halves(grad_kv), halves(attended))
+    kept = jnp.concatenate(kept, axis=1)
+    arrived = swap_cores(jnp.concatenate(sent, axis=1))
+    split = grad_query.shape[-1] // 2 + grad_kv.shape[-1] // 2
+    left = jnp.concatenate([kept, arrived], axis=0)
     contract_rows = (((0,), (0,)), ((), ()))
-    ctx_count = lax.axis_size("ctx")
-    fsdp_count = lax.axis_size("fsdp")
     term_in = lax.dot_general(
-        hidden_rows, left_rows, contract_rows, preferred_element_type=jnp.float32
+        both_in, left[:, :split], contract_rows, preferred_element_type=jnp.float32
     )
     term_out = 2.0 * lax.dot_general(
-        cot_rows, attended_rows, contract_rows, preferred_element_type=jnp.float32
-    )
-    summed = lax.psum_scatter(
-        jnp.concatenate([term_in, term_out], axis=1),
-        ("ctx", "fsdp"),
-        scatter_dimension=0,
-        tiled=True,
-    )
-    token_total = seq_count * shard * ctx_count * fsdp_count
-    grad_weights = summed * (1.0 / math.sqrt(token_total))
+        both_out, left[:, split:], contract_rows, preferred_element_type=jnp.float32
+    )
+    terms = jnp.concatenate([term_in, term_out], axis=1).astype(jnp.bfloat16)
+    chips = lax.axis_size(CHIPS)
+    terms = terms.reshape(chips, width // chips, -1)
+    terms = lax.all_to_all(terms, CHIPS, 0, 0)
+    summed = jnp.sum(terms.astype(jnp.float32), axis=0) * (1.0 / math.sqrt(token_total))
+    mine = summed.shape[0] // 2
+    upper = jnp.where(core == 0, summed[:mine], summed[mine:])
+    lower = swap_cores(jnp.where(core == 0, summed[mine:], summed[:mine]))
+    zero = jnp.where(core == 0, upper, lower)
+    one = jnp.where(core == 0, lower, upper)
+    q_half = grad_query.shape[-1] // 2
+    grad_weights = jnp.concatenate(
+        [
+            zero[:, :q_half],
+            one[:, :q_half],
+            zero[:, q_half:split],
+            one[:, q_half:split],
+            zero[:, split:],
+            one[:, split:],
+        ],
+        axis=1,
+    )
     return (x_prev, grad_cur, grad_weights)
 
 
 def solution(mesh):
+    mesh = Mesh(mesh.devices.reshape(4, 4, 2, 2, 2), CTX + FSDP)
     in_specs = (
-        P("fsdp", "ctx", None),
-        P("fsdp", "ctx", None),
-        P("fsdp", "ctx", None),
-        P("fsdp", "ctx", None),
-        P("fsdp", None),
-        P("fsdp", None),
-        P("fsdp", None),
-    )
-    out_specs = (P("fsdp", "ctx", None), P("fsdp", "ctx", None), P(("ctx", "fsdp"), None))
+        P(FSDP, CTX, None),
+        P(FSDP, CTX, None),
+        P(FSDP, CTX, None),
+        P(FSDP, CTX, None),
+        P(FSDP, None),
+        P(FSDP, None),
+        P(FSDP, None),
+    )
+    out_specs = (P(FSDP, CTX, None), P(FSDP, CTX, None), P(CTX + FSDP, None))
     return jax.shard_map(shards, mesh=mesh, in_specs=in_specs, out_specs=out_specs, check_vma=False)

time: 946 us -> 316 us (0.33)
  waiting for transfers between devices: 797 us -> 175 us
  local copies, waits for them, and re-layouts: 32.1 us -> 7.93 us
  starting transfers between devices: 20.6 us -> 34.9 us
    unnamed x5 -> x3, waiting for transfers between devices: 683 us -> 2.06 us
    all_to_all x0 -> x1, waiting for transfers between devices: none -> 57.9 us  [shards(): terms = lax.all_to_all(terms, CHIPS, 0, 0)]
    unnamed x22 -> x28, local copies, waits for them, and re-layouts: 24.2 us -> 1.01 us
    all_to_all x0 -> x1, starting transfers between devices: none -> 13.6 us  [shards(): terms = lax.all_to_all(terms, CHIPS, 0, 0)]
  transfers between devices with their start and end apart: 12 -> 16, of which waited for: 11 -> 13; matrix products, arithmetic and copies ran while one was open for 2% -> 25% of each run, Pallas kernels for 0% -> 0%
where the time goes in v1:
time: 316 us; the launch traced here: 310 us
  waiting for transfers between devices  175 us (55%)
  matrix products  54.2 us (17%)
  starting transfers between devices  34.9 us (11%)
  other arithmetic  24.2 us (8%)
  between operations  14.2 us (4%)
  local copies, waits for them, and re-layouts  7.93 us (3%)
    all_to_all x1, waiting for transfers between devices, shards(): terms = lax.all_to_all(terms, CHIPS, 0, 0)  57.9 us
    all_gather x1, waiting for transfers between devices, shards(): lax.all_gather(w_q, FSDP, axis=0, tiled=True)  37.6 us
    ppermute x8, waiting for transfers between devices, from_behind(): lax.ppermute(value, axis, [(source, source + steps) for source in range(l...  32.7 us
    all_gather x1, waiting for transfers between devices, shards(): lax.all_gather(w_kv, FSDP, axis=0, tiled=True)  28.7 us
    ppermute x8, starting transfers between devices, from_behind(): lax.ppermute(value, axis, [(source, source + steps) for source in range(l...  20.3 us
    all_gather x1, waiting for transfers between devices, shards(): lax.all_gather(w_out, FSDP, axis=0, tiled=True)  14.1 us
    all_to_all x1, starting transfers between devices, shards(): terms = lax.all_to_all(terms, CHIPS, 0, 0)  13.6 us
    sub x2, matrix products, head_block(): expo = jnp.exp(scores - top)  10.4 us
  transfers between devices with their start and end apart: 16, of which 13 were waited for; matrix products, arithmetic and copies ran while one was open for 25% of the time, Pallas kernels for 0%

profile of v1, /device:TPU:0, one launch (start us, length us, event | category | flops | bytes accessed | tf_op | source)
XLA Modules:
  0.0 310.2 jit_solution(6684000862140531037)
XLA Ops:
  10.1 28.7 %all-gather.4.cloned.1.call-done = bf16[2048,512]{1,0:T(8,128)(2,1)} async-done(((bf16[512,512]{1,0:T(8,128)(2,1)}), bf16[2048,512]{1,0:T(8,128)(2,1)}) %all-gather.4.cloned.1.call-update) | async-done | bytes 2097168 | tf_op jit(solution)/shard_map/all_gather | solution.py:108
  38.8 2.3 fusion.77
  41.1 5.1 %collective-permute-start = (bf16[1,256,512]{2,1,0:T(8,128)(2,1)S(1)}, bf16[1,256,512]{2,1,0:T(8,128)(2,1)S(1)}, u32[]{:S(2)}, u32[]{:S(2)}) collective-permute-start(bf16[1,256,512]{2,1,0:T(8,128)(2,1)S(1)} %fusion.77), channel_id=1, source_target_pairs={{0,16},{4,20},{8,24},{12,28},{16,32},{20,36},{24,40},{28,44},{32,4... | collective-permute-start | bytes 786440 | tf_op jit(solution)/shard_map/ppermute | solution.py:25
  46.2 2.6 collective-permute-start.1
  48.8 2.5 collective-permute-start.2
  51.4 4.9 %collective-permute-start.3 = (bf16[1,256,512]{2,1,0:T(8,128)(2,1)S(1)}, bf16[1,256,512]{2,1,0:T(8,128)(2,1)S(1)}, u32[]{:S(2)}, u32[]{:S(2)}) collective-permute-start(bf16[1,256,512]{2,1,0:T(8,128)(2,1)S(1)} %fusion.77), channel_id=1, source_target_pairs={{0,4},{4,8},{8,12},{12,16},{16,20},{20,24},{24,28},{28,32},{32,36}... | collective-permute-start | bytes 786440 | tf_op jit(solution)/shard_map/ppermute | solution.py:25
  56.4 3.8 %collective-permute-done.1 = bf16[1,256,512]{2,1,0:T(8,128)(2,1)S(1)} collective-permute-done((bf16[1,256,512]{2,1,0:T(8,128)(2,1)S(1)}, bf16[1,256,512]{2,1,0:T(8,128)(2,1)S(1)}, u32[]{:S(2)}, u32[]{:S(2)}) %collective-permute-start.1) | collective-permute-done | bytes 262176 | tf_op jit(solution)/shard_map/ppermute | solution.py:25
  60.2 6.3 %collective-permute-done.2 = bf16[1,256,512]{2,1,0:T(8,128)(2,1)S(1)} collective-permute-done((bf16[1,256,512]{2,1,0:T(8,128)(2,1)S(1)}, bf16[1,256,512]{2,1,0:T(8,128)(2,1)S(1)}, u32[]{:S(2)}, u32[]{:S(2)}) %collective-permute-start.2) | collective-permute-done | bytes 262176 | tf_op jit(solution)/shard_map/ppermute | solution.py:25
  66.5 3.9 %collective-permute-done.3 = bf16[1,256,512]{2,1,0:T(8,128)(2,1)S(1)} collective-permute-done((bf16[1,256,512]{2,1,0:T(8,128)(2,1)S(1)}, bf16[1,256,512]{2,1,0:T(8,128)(2,1)S(1)}, u32[]{:S(2)}, u32[]{:S(2)}) %collective-permute-start.3) | collective-permute-done | bytes 262176 | tf_op jit(solution)/shard_map/ppermute | solution.py:25
  72.6 14.1 %all-gather.8.cloned.1.call-done = bf16[2048,1024]{1,0:T(8,128)(2,1)} async-done(((bf16[512,1024]{1,0:T(8,128)(2,1)}), bf16[2048,1024]{1,0:T(8,128)(2,1)}) %all-gather.8.cloned.1.call-update) | async-done | bytes 4194320 | tf_op jit(solution)/shard_map/all_gather | solution.py:109
  86.7 3.8 %fusion.76 = bf16[256,1024]{1,0:T(8,128)(2,1)S(1)} fusion(bf16[2048,1024]{1,0:T(8,128)(2,1)} %all-gather.8.cloned.1.call-done, bf16[1,256,2048]{2,1,0:T(8,128)(2,1)} %param.12), kind=kOutput, calls=%fused_computation.93 | convolution fusion | flops 1074266112 | bytes 5767168 | tf_op jit(solution)/shard_map/sid,dc->sic/dot_general | solution.py:123
  90.8 37.6 %all-gather.6.cloned.1.call-done = bf16[2048,1024]{1,0:T(8,128)(2,1)} async-done(((bf16[512,1024]{1,0:T(8,128)(2,1)}), bf16[2048,1024]{1,0:T(8,128)(2,1)}) %all-gather.6.cloned.1.call-update) | async-done | bytes 4194320 | tf_op jit(solution)/shard_map/all_gather | solution.py:107
  128.4 3.4 %convolution_convert_fusion.2 = bf16[256,1024]{1,0:T(8,128)(2,1)S(1)} fusion(bf16[256,2048]{1,0:T(8,128)(2,1)S(1)} %fusion.78, bf16[2048,1024]{1,0:T(8,128)(2,1)} %all-gather.6.cloned.1.call-done), kind=kOutput, calls=%fused_computation.94 | convolution fusion | flops 1074003968 | bytes 5767168 | tf_op jit(solution)/shard_map/sid,dc->sic/dot_general | solution.py:116
  132.2 1.2 copy_bitcast_fusion
  133.4 46.7 %while.29 = (s32[]{:T(128)}, bf16[2,256,4,128]{1,3,2,0:T(8,128)(2,1)}, bf16[2,256,4,128]{1,3,2,0:T(8,128)(2,1)}, bf16[2,1280,128]{1,2,0:T(8,128)(2,1)}, bf16[2,1...) while((s32[]{:T(128)}, ...), condition=%wide.region_4.5_spmd.clone, body=%wide.region_1.4_spmd.clone.sunk | while | flops 2030305536 | bytes 57441732 | solution.py:90
  135.5 5.2 %exponential_reduce_fusion.2 = (f32[4,256]{1,0:T(4,128)S(1)}, f32[4,256,1280]{1,2,0:T(8,128)}) fusion(pred[256,1280]{0,1:T(8,128)(4,1)S(1)} %fusion.142, bf16[2,1280,128]{2,1,0:T(8,128)(2,1)} %get-tuple-element.280, s32[]{:T(128)S(6)} %copy.69, bf16[2,256,4,128]{3,1,2,0:T(8,128)(2,1)} %get-tuple-element.281), kind=kOutput, calls=%fused_computation.9.clone.1 | convolution fusion | flops 340788480 | bytes 6165504 | tf_op jit(solution)/shard_map/while/body/eval_jaxpr/while/body/eval_jaxpr/sub | solution.py:44
  140.7 4.0 %fusion.143 = bf16[4,256,1280]{1,2,0:T(8,128)(2,1)S(1)} fusion(f32[4,256]{1,0:T(4,128)S(1)} %get-tuple-element.242, f32[4,256,1280]{1,2,0:T(8,128)} %get-tuple-element.243), kind=kLoop, calls=%fused_computation.18.clone.1 | loop fusion | flops 2621440 | bytes 7868416 | tf_op jit(solution)/shard_map/while/body/eval_jaxpr/while/body/eval_jaxpr/convert_element_type | solution.py:46
  144.7 1.9 fusion.148
  146.6 2.2 fusion.144
  148.9 2.5 fusion.146
  151.6 1.8 fusion.149
  153.4 2.2 fusion.147
  158.9 5.2 %exponential_reduce_fusion.2 = (f32[4,256]{1,0:T(4,128)S(1)}, f32[4,256,1280]{1,2,0:T(8,128)}) fusion(pred[256,1280]{0,1:T(8,128)(4,1)S(1)} %fusion.142, bf16[2,1280,128]{2,1,0:T(8,128)(2,1)} %get-tuple-element.280, s32[]{:T(128)S(6)} %copy.69, bf16[2,256,4,128]{3,1,2,0:T(8,128)(2,1)} %get-tuple-element.281), kind=kOutput, calls=%fused_computation.9.clone.1 | convolution fusion | flops 340788480 | bytes 6165504 | tf_op jit(solution)/shard_map/while/body/eval_jaxpr/while/body/eval_jaxpr/sub | solution.py:44
  164.1 4.0 %fusion.143 = bf16[4,256,1280]{1,2,0:T(8,128)(2,1)S(1)} fusion(f32[4,256]{1,0:T(4,128)S(1)} %get-tuple-element.242, f32[4,256,1280]{1,2,0:T(8,128)} %get-tuple-element.243), kind=kLoop, calls=%fused_computation.18.clone.1 | loop fusion | flops 2621440 | bytes 7868416 | tf_op jit(solution)/shard_map/while/body/eval_jaxpr/while/body/eval_jaxpr/convert_element_type | solution.py:46
  168.1 1.9 fusion.148
  170.0 2.2 fusion.144
  172.3 2.5 fusion.146
  175.0 1.8 fusion.149
  176.8 2.3 fusion.147
  180.1 1.4 maximum_bitcast_fusion
  181.6 1.3 collective-permute-start.4
  182.9 1.3 collective-permute-start.7
  184.2 1.3 collective-permute-start.6
  185.5 1.3 collective-permute-start.5
  189.0 2.9 collective-permute-done.4
  191.9 3.5 %collective-permute-done.7 = bf16[1,256,512]{1,2,0:T(8,128)(2,1)S(1)} collective-permute-done((bf16[1,256,512]{1,2,0:T(8,128)(2,1)S(1)}, bf16[1,256,512]{1,2,0:T(8,128)(2,1)S(1)}, u32[]{:S(2)}, u32[]{:S(2)}) %collective-permute-start.7) | collective-permute-done | bytes 262176 | tf_op jit(solution)/shard_map/ppermute | solution.py:25
  195.5 7.3 %collective-permute-done.6 = bf16[1,256,512]{1,2,0:T(8,128)(2,1)S(1)} collective-permute-done((bf16[1,256,512]{1,2,0:T(8,128)(2,1)S(1)}, bf16[1,256,512]{1,2,0:T(8,128)(2,1)S(1)}, u32[]{:S(2)}, u32[]{:S(2)}) %collective-permute-start.6) | collective-permute-done | bytes 262176 | tf_op jit(solution)/shard_map/ppermute | solution.py:25
  202.7 5.0 %collective-permute-done.5 = bf16[1,256,512]{1,2,0:T(8,128)(2,1)S(1)} collective-permute-done((bf16[1,256,512]{1,2,0:T(8,128)(2,1)S(1)}, bf16[1,256,512]{1,2,0:T(8,128)(2,1)S(1)}, u32[]{:S(2)}, u32[]{:S(2)}) %collective-permute-start.5) | collective-permute-done | bytes 262176 | tf_op jit(solution)/shard_map/ppermute | solution.py:25
  208.7 1.6 collective-permute-done.9
  210.3 2.9 multiply_convert_fusion
  213.3 1.9 convolution_convert_fusion.1
  215.2 2.8 pad_maximum_fusion
  217.9 13.6 %all-to-all-start = ((bf16[64,32,1280]{2,1,0:T(8,128)(2,1)}), bf16[64,32,1280]{2,1,0:T(8,128)(2,1)}, u32[]{:S(2)}, u32[]{:S(2)}) async-start(bf16[64,32,1280]{2,1,0:T(8,128)(2,1)} %pad_maximum_fusion), calls=%async_computation | async-start | bytes 10485760 | tf_op jit(solution)/shard_map/all_to_all | solution.py:185
  231.6 3.8 %fusion.96 = f32[256,2048]{1,0:T(8,128)S(1)} fusion(bf16[256,1024]{0,1:T(8,128)(2,1)} %bitcast.15, bf16[2048,1024]{1,0:T(8,128)(2,1)} %all-gather.6.cloned.1.call-done), kind=kOutput, calls=%fused_computation.144 | convolution fusion | flops 1073741824 | bytes 6815744 | tf_op jit(solution)/shard_map/sic,dc->sid/dot_general | solution.py:146
  235.5 3.5 %fusion.63 = bf16[1,256,2048]{2,1,0:T(8,128)(2,1)} fusion(bf16[256,1024]{0,1:T(8,128)(2,1)} %bitcast.12, bf16[2048,1024]{1,0:T(8,128)(2,1)S(1)} %copy-done.7, bf16[1,256,2048]{2,1,0:T(8,128)(2,1)S(1)} %copy-done.8), kind=kOutput, calls=%fused_computation.77 | convolution fusion | flops 1075838976 | bytes 6815744 | tf_op jit(solution)/shard_map/sic,dc->sid/dot_general | solution.py:144
  240.0 57.9 %all-to-all-done = bf16[64,32,1280]{2,1,0:T(8,128)(2,1)} async-done(((bf16[64,32,1280]{2,1,0:T(8,128)(2,1)}), bf16[64,32,1280]{2,1,0:T(8,128)(2,1)}, u32[]{:S(2)}, u32[]{:S(2)}) %all-to-all-start) | async-done | bytes 5242912 | tf_op jit(solution)/shard_map/all_to_all | solution.py:185
  297.8 3.4 %convert_reduce_fusion = f32[32,1280]{1,0:T(8,128)S(1)} fusion(bf16[64,32,1280]{2,1,0:T(8,128)(2,1)} %all-to-all-done), kind=kLoop, calls=%fused_computation.63 | loop fusion | flops 5201920 | bytes 5406720 | tf_op jit(solution)/shard_map/reduce_sum | solution.py:186
  301.3 1.6 fusion.68
  (94 shorter events, 18.1 us)
Async XLA Ops:
  7.2 2.3 copy-start
  7.2 31.6 %all-gather.4.cloned.1.call-start = ((), (), s32[]{:S(2)}) async-start(), calls=%async_computation.1 | async-start | bytes 2621440 | tf_op jit(solution)/shard_map/all_gather | solution.py:108
  7.9 78.7 %all-gather.8.cloned.1.call-start = ((), (), s32[]{:S(2)}) async-start(), calls=%async_computation.3 | async-start | bytes 5242880 | tf_op jit(solution)/shard_map/all_gather | solution.py:109
  8.7 119.7 %all-gather.6.cloned.1.call-start = ((), (), s32[]{:S(2)}) async-start(), calls=%async_computation.2 | async-start | bytes 5242880 | tf_op jit(solution)/shard_map/all_gather | solution.py:107
  9.4 199.3 %collective-permute-start.10 = (bf16[256,2048]{1,0:T(8,128)(2,1)}, bf16[256,2048]{1,0:T(8,128)(2,1)}, u32[]{:S(2)}, u32[]{:S(2)}) collective-permute-start(bf16[256,2048]{1,0:T(8,128)(2,1)} %bitcast.9), channel_id=1, source_target_pairs={{0,1},{1,0},{2,3},{3,2},{4,5},{5,4},{6,7},{7,6},{8,9},{9,8},{10,11... | collective-permute-start | bytes 3145736 | tf_op jit(solution)/shard_map/ppermute | solution.py:29
  10.1 118.3 %copy-start.4 = (bf16[256,2048]{1,0:T(8,128)(2,1)}, bf16[256,2048]{1,0:T(8,128)(2,1)S(1)}, u32[]{:S(2)}) copy-start(bf16[256,2048]{1,0:T(8,128)(2,1)S(1)} %fusion.78) | copy-start | bytes 3145732
  41.1 15.3 %collective-permute-start = (bf16[1,256,512]{2,1,0:T(8,128)(2,1)S(1)}, bf16[1,256,512]{2,1,0:T(8,128)(2,1)S(1)}, u32[]{:S(2)}, u32[]{:S(2)}) collective-permute-start(bf16[1,256,512]{2,1,0:T(8,128)(2,1)S(1)} %fusion.77), channel_id=1, source_target_pairs={{0,16},{4,20},{8,24},{12,28},{16,32},{20,36},{24,40},{28,44},{32,4... | collective-permute-start | bytes 786440 | tf_op jit(solution)/shard_map/ppermute | solution.py:25
  46.2 14.0 %collective-permute-start.1 = (bf16[1,256,512]{2,1,0:T(8,128)(2,1)S(1)}, bf16[1,256,512]{2,1,0:T(8,128)(2,1)S(1)}, u32[]{:S(2)}, u32[]{:S(2)}) collective-permute-start(bf16[1,256,512]{2,1,0:T(8,128)(2,1)S(1)} %fusion.77), channel_id=1, source_target_pairs={{0,12},{4,16},{8,20},{12,24},{16,28},{20,32},{24,36},{28,40},{32,4... | collective-permute-start | bytes 786440 | tf_op jit(solution)/shard_map/ppermute | solution.py:25
  48.8 17.7 %collective-permute-start.2 = (bf16[1,256,512]{2,1,0:T(8,128)(2,1)S(1)}, bf16[1,256,512]{2,1,0:T(8,128)(2,1)S(1)}, u32[]{:S(2)}, u32[]{:S(2)}) collective-permute-start(bf16[1,256,512]{2,1,0:T(8,128)(2,1)S(1)} %fusion.77), channel_id=1, source_target_pairs={{0,8},{4,12},{8,16},{12,20},{16,24},{20,28},{24,32},{28,36},{32,40... | collective-permute-start | bytes 786440 | tf_op jit(solution)/shard_map/ppermute | solution.py:25
  51.4 19.1 %collective-permute-start.3 = (bf16[1,256,512]{2,1,0:T(8,128)(2,1)S(1)}, bf16[1,256,512]{2,1,0:T(8,128)(2,1)S(1)}, u32[]{:S(2)}, u32[]{:S(2)}) collective-permute-start(bf16[1,256,512]{2,1,0:T(8,128)(2,1)S(1)} %fusion.77), channel_id=1, source_target_pairs={{0,4},{4,8},{8,12},{12,16},{16,20},{20,24},{24,28},{28,32},{32,36}... | collective-permute-start | bytes 786440 | tf_op jit(solution)/shard_map/ppermute | solution.py:25
  140.7 8.2 %slice-start = ((s8[5242880]{0:T(1024)(128)(4,1)}), s8[4194304]{0:T(1024)(128)(4,1)S(1)}, s32[]{:S(2)}) async-start(s8[5242880]{0:T(1024)(128)(4,1)} %bitcast.206), calls=%async_computation.4 | async-start | bytes 8388608 | tf_op jit(solution)/shard_map/while/body/eval_jaxpr/while
  144.7 4.2 %slice-start.1 = ((s8[5242880]{0:T(1024)(128)(4,1)}), s8[1048576]{0:T(1024)(128)(4,1)S(1)}, s32[]{:S(2)}) async-start(s8[5242880]{0:T(1024)(128)(4,1)} %bitcast.206), calls=%async_computation.5 | async-start | bytes 2097152 | tf_op jit(solution)/shard_map/while/body/eval_jaxpr/while
  164.1 8.2 %slice-start = ((s8[5242880]{0:T(1024)(128)(4,1)}), s8[4194304]{0:T(1024)(128)(4,1)S(1)}, s32[]{:S(2)}) async-start(s8[5242880]{0:T(1024)(128)(4,1)} %bitcast.206), calls=%async_computation.4 | async-start | bytes 8388608 | tf_op jit(solution)/shard_map/while/body/eval_jaxpr/while
  168.1 4.2 %slice-start.1 = ((s8[5242880]{0:T(1024)(128)(4,1)}), s8[1048576]{0:T(1024)(128)(4,1)S(1)}, s32[]{:S(2)}) async-start(s8[5242880]{0:T(1024)(128)(4,1)} %bitcast.206), calls=%async_computation.5 | async-start | bytes 2097152 | tf_op jit(solution)/shard_map/while/body/eval_jaxpr/while
  181.6 10.3 %collective-permute-start.4 = (bf16[1,256,512]{1,2,0:T(8,128)(2,1)S(1)}, bf16[1,256,512]{1,2,0:T(8,128)(2,1)S(1)}, u32[]{:S(2)}, u32[]{:S(2)}) collective-permute-start(bf16[1,256,512]{1,2,0:T(8,128)(2,1)S(1)} %get-tuple-element.145), channel_id=1, source_target_pairs={{4,0},{8,4},{12,8},{16,12},{20,16},{24,20},{28,24},{32,28},{36,32}... | collective-permute-start | bytes 786440 | tf_op jit(solution)/shard_map/ppermute | solution.py:25
  182.9 12.6 %collective-permute-start.7 = (bf16[1,256,512]{1,2,0:T(8,128)(2,1)S(1)}, bf16[1,256,512]{1,2,0:T(8,128)(2,1)S(1)}, u32[]{:S(2)}, u32[]{:S(2)}) collective-permute-start(bf16[1,256,512]{1,2,0:T(8,128)(2,1)S(1)} %get-tuple-element.146), channel_id=1, source_target_pairs={{16,0},{20,4},{24,8},{28,12},{32,16},{36,20},{40,24},{44,28},{48,3... | collective-permute-start | bytes 786440 | tf_op jit(solution)/shard_map/ppermute | solution.py:25
  184.2 18.6 %collective-permute-start.6 = (bf16[1,256,512]{1,2,0:T(8,128)(2,1)S(1)}, bf16[1,256,512]{1,2,0:T(8,128)(2,1)S(1)}, u32[]{:S(2)}, u32[]{:S(2)}) collective-permute-start(bf16[1,256,512]{1,2,0:T(8,128)(2,1)S(1)} %get-tuple-element.147), channel_id=1, source_target_pairs={{12,0},{16,4},{20,8},{24,12},{28,16},{32,20},{36,24},{40,28},{44,3... | collective-permute-start | bytes 786440 | tf_op jit(solution)/shard_map/ppermute | solution.py:25
  185.5 22.2 %collective-permute-start.5 = (bf16[1,256,512]{1,2,0:T(8,128)(2,1)S(1)}, bf16[1,256,512]{1,2,0:T(8,128)(2,1)S(1)}, u32[]{:S(2)}, u32[]{:S(2)}) collective-permute-start(bf16[1,256,512]{1,2,0:T(8,128)(2,1)S(1)} %get-tuple-element.148), channel_id=1, source_target_pairs={{8,0},{12,4},{16,8},{20,12},{24,16},{28,20},{32,24},{36,28},{40,32... | collective-permute-start | bytes 786440 | tf_op jit(solution)/shard_map/ppermute | solution.py:25
  187.8 20.4 %copy-start.5 = (bf16[256,2048]{1,0:T(8,128)(2,1)S(1)}, bf16[256,2048]{1,0:T(8,128)(2,1)}, u32[]{:S(2)}) copy-start(bf16[256,2048]{1,0:T(8,128)(2,1)} %copy-done.4) | copy-start | bytes 3145732
  208.0 2.4 collective-permute-start.9
  208.2 5.1 %collective-permute-start.8 = (bf16[256,2048]{1,0:T(8,128)(2,1)S(1)}, bf16[256,2048]{1,0:T(8,128)(2,1)S(1)}, u32[]{:S(2)}, u32[]{:S(2)}) collective-permute-start(bf16[256,2048]{1,0:T(8,128)(2,1)S(1)} %copy-done.5), channel_id=1, source_target_pairs={{0,1},{1,0},{2,3},{3,2},{4,5},{5,4},{6,7},{7,6},{8,9},{9,8},{10,11... | collective-permute-start | bytes 3145736 | tf_op jit(solution)/shard_map/ppermute | solution.py:29
  217.9 79.9 %all-to-all-start = ((bf16[64,32,1280]{2,1,0:T(8,128)(2,1)}), bf16[64,32,1280]{2,1,0:T(8,128)(2,1)}, u32[]{:S(2)}, u32[]{:S(2)}) async-start(bf16[64,32,1280]{2,1,0:T(8,128)(2,1)} %pad_maximum_fusion), calls=%async_computation | async-start | bytes 10485760 | tf_op jit(solution)/shard_map/all_to_all | solution.py:185
  231.6 3.8 %copy-start.7 = (bf16[2048,1024]{1,0:T(8,128)(2,1)S(1)}, bf16[2048,1024]{1,0:T(8,128)(2,1)}, u32[]{:S(2)}) copy-start(bf16[2048,1024]{1,0:T(8,128)(2,1)} %all-gather.8.cloned.1.call-done) | copy-start | bytes 12582916
  231.6 3.9 %copy-start.8 = (bf16[1,256,2048]{2,1,0:T(8,128)(2,1)S(1)}, bf16[1,256,2048]{2,1,0:T(8,128)(2,1)}, u32[]{:S(2)}) copy-start(bf16[1,256,2048]{2,1,0:T(8,128)(2,1)} %param.10) | copy-start | bytes 3145732
  235.5 3.5 %copy-start.1 = (bf16[1,256,2048]{2,1,0:T(8,128)(2,1)S(1)}, bf16[1,256,2048]{2,1,0:T(8,128)(2,1)}, u32[]{:S(2)}) copy-start(bf16[1,256,2048]{2,1,0:T(8,128)(2,1)} %param.9) | copy-start | bytes 3145732
  235.5 3.5 %copy-start.2 = (bf16[2048,512]{1,0:T(8,128)(2,1)S(1)}, bf16[2048,512]{1,0:T(8,128)(2,1)}, u32[]{:S(2)}) copy-start(bf16[2048,512]{1,0:T(8,128)(2,1)} %all-gather.4.cloned.1.call-done) | copy-start | bytes 6291460
  297.8 3.5 %copy-start.3 = (bf16[1,256,2048]{2,1,0:T(8,128)(2,1)S(1)}, bf16[1,256,2048]{2,1,0:T(8,128)(2,1)}, u32[]{:S(2)}) copy-start(bf16[1,256,2048]{2,1,0:T(8,128)(2,1)} %param.11) | copy-start | bytes 3145732
  301.2 1.7 collective-permute-start.11
  303.0 0.7 copy-start.6
Sparse Core Ops, SparseCore 0:
  9.7 29.0 all-gather.3
  40.5 46.1 all-gather.7
  88.3 39.9 all-gather.5

commit v2 on v0

v2 whole, which is shorter than its diff:
```python
import math

import jax
import jax.numpy as jnp
from jax import lax
from jax.experimental import pallas as pl
from jax.experimental.pallas import tpu as pltpu
from jax.sharding import Mesh
from jax.sharding import PartitionSpec as P

QUERY_HEADS = 8
KEY_VALUE_HEADS = 2
HEAD_SIZE = 128
WINDOW_TOKENS = 1024
GROUP = QUERY_HEADS // KEY_VALUE_HEADS
SCALE = 1.0 / math.sqrt(HEAD_SIZE)
LANES = 128
EPS = 1e-05

CTX = ("x", "z", "yl")
FSDP = ("yh", "c")
CHIPS = ("x", "z", "yl", "yh")
QUARTERS = (0, 3, 1, 2)

F32 = jnp.float32
BF16 = jnp.bfloat16
VMEM = pl.BlockSpec(memory_space=pltpu.VMEM)
SMEM = pl.BlockSpec(memory_space=pltpu.SMEM)


def call(kernel, outs, n_scalar, args, flops, scratch=(), limit=24):
    moved = sum(a.size * a.dtype.itemsize for a in args) + sum(
        math.prod(o.shape) * o.dtype.itemsize for o in outs
    )
    return pl.pallas_call(
        kernel,
        out_shape=outs,
        in_specs=[SMEM] * n_scalar + [VMEM] * (len(args) - n_scalar),
        out_specs=[VMEM] * len(outs),
        scratch_shapes=list(scratch),
        cost_estimate=pl.CostEstimate(flops=flops, bytes_accessed=moved, transcendentals=0),
        compiler_params=pltpu.CompilerParams(vmem_limit_bytes=limit * 2**20),
    )(*args)


def array(shape, dtype):
    return jax.ShapeDtypeStruct(shape, dtype)


def dot(a, b, dims):
    return lax.dot_general(a, b, (dims, ((), ())), preferred_element_type=F32)


NN = ((1,), (0,))
NT = ((1,), (1,))


def swap_cores(value):
    return lax.ppermute(value, "c", [(0, 1), (1, 0)])


def swap_low(value):
    return lax.ppermute(value, "yl", [(0, 1), (1, 0)])


def along(value, axis, step):
    count = lax.axis_size(axis)
    return lax.ppermute(value, axis, [(i, (i + step) % count) for i in range(count)])


def shift(value, step):
    count = lax.axis_size(("x", "z"))
    pairs = [(i, i + step) for i in range(count) if 0 <= i + step < count]
    return lax.ppermute(value, ("x", "z"), pairs)


def fetch(value):
    return lax.ppermute(value, ("yl", "yh"), [(0, 3), (3, 0), (1, 2), (2, 1)])


def gather_kv(shard):
    far = fetch(shard)
    other = swap_cores(shard)
    return (shard, other, far, swap_cores(far))


def gather_qo(w_q, w_out, colour):
    rows = w_q.shape[0] // 4
    piece = jnp.concatenate(
        [lax.dynamic_slice_in_dim(w, colour * rows, rows, 0) for w in (w_q, w_out)], axis=1
    )
    piece = fetch(piece)
    left = along(piece, "x", 1)
    right = along(piece, "x", -1)
    ahead = along(piece, "z", -1)
    shard = jnp.concatenate([w_q, w_out], axis=1)
    other = swap_cores(shard)
    far = jnp.concatenate([piece, left, right, ahead], axis=0)
    return (shard, other, far, swap_cores(far))


def normalize(x):
    values = x.astype(F32)
    inv_rms = lax.rsqrt(jnp.mean(values * values, axis=-1, keepdims=True) + EPS)
    return values * inv_rms, inv_rms


def block(place, j):
    return pl.ds(pl.multiple_of(place[j] * LANES, LANES), LANES)


def whole(place, i, depth):
    return pl.ds(pl.multiple_of(place[16 + i] * depth, depth), depth)


def prepare_kernel(place, x_ref, c_ref, hidden_ref, hp_ref, cp_ref, ht_ref, ct_ref):
    normed, _ = normalize(x_ref[...])
    hidden_ref[...] = normed.astype(BF16)
    for j in range(hp_ref.shape[1] // LANES):
        to = slice(j * LANES, (j + 1) * LANES)
        hp_ref[:, to] = hidden_ref[:, block(place, j)]
        cp_ref[:, to] = c_ref[:, block(place, j)]
        ht_ref[to, :] = hidden_ref[:, to].T
        ct_ref[to, :] = c_ref[:, to].T


def project(rows_ref, shards, columns):
    depth = shards[0].shape[0]
    total = None
    for i, shard in enumerate(shards):
        term = dot(rows_ref[:, i * depth : (i + 1) * depth], shard[:, columns], NN)
        total = term if total is None else total + term
    return total


def kv_kernel(place, hidden_ref, s0, s1, s2, s3, out_ref):
    depth = s0.shape[0]
    total = None
    for i, shard in enumerate((s0, s1, s2, s3)):
        term = dot(hidden_ref[:, whole(place, i, depth)], shard[...], NN)
        total = term if total is None else total + term
    out_ref[...] = total.astype(BF16)


def query_kernel(hp_ref, cp_ref, s0, s1, s2, s3, q_ref, g_ref):
    width = q_ref.shape[1]
    shards = (s0, s1, s2, s3)
    q_ref[...] = project(hp_ref, shards, slice(0, width)).astype(BF16)
    g_ref[...] = (2.0 * project(cp_ref, shards, slice(width, 2 * width))).astype(BF16)


def attention_kernel(
    where, q_ref, g_ref, k4, k3, k2, k1, k0,
    att_ref, dq_ref, t4, t3, t2, t1, t0,
    kt_ref, vt_ref, e_ref, dk_ref, dv_ref,
):
    shard = q_ref.shape[0]
    ctx, group = where[0], where[1]
    pieces, terms = (k4, k3, k2, k1, k0), (t4, t3, t2, t1, t0)
    count = len(pieces)
    log2e = SCALE * math.log2(math.e)
    key = lax.broadcasted_iota(jnp.int32, (shard, shard), 0)
    query = lax.broadcasted_iota(jnp.int32, (shard, shard), 1)
    kcol = pl.ds(pl.multiple_of(group * HEAD_SIZE, HEAD_SIZE), HEAD_SIZE)
    vcol = pl.ds(pl.multiple_of((KEY_VALUE_HEADS + group) * HEAD_SIZE, HEAD_SIZE), HEAD_SIZE)
    for b, piece in enumerate(pieces):
        rows = slice(b * shard, (b + 1) * shard)
        kt_ref[:, rows] = piece[:, kcol].T
        vt_ref[:, rows] = piece[:, vcol].T
    dk_ref[...] = jnp.zeros_like(dk_ref)
    dv_ref[...] = jnp.zeros_like(dv_ref)

    @pl.loop(0, GROUP)
    def _(m):
        column = pl.ds(pl.multiple_of((group * GROUP + m) * HEAD_SIZE, HEAD_SIZE), HEAD_SIZE)
        q, grad = q_ref[:, column], g_ref[:, column]
        top = None
        for b, piece in enumerate(pieces):
            s = dot(piece[:, kcol], q, NT)
            if b == 0:
                s = jnp.where(key > query, s, -jnp.inf)
            if b == count - 1:
                s = jnp.where(key <= query, s, -jnp.inf)
            e_ref[b * shard : (b + 1) * shard, :] = s
            best = jnp.max(s, axis=0, keepdims=True)
            if b < count - 1:
                best = jnp.where(ctx >= count - 1 - b, best, -jnp.inf)
            top = best if top is None else jnp.maximum(top, best)
        total = None
        for b in range(count):
            rows = slice(b * shard, (b + 1) * shard)
            base = top * log2e
            if b < count - 1:
                base = jnp.where(ctx >= count - 1 - b, base, jnp.inf)
            e = jnp.exp2(e_ref[rows, :] * log2e - base)
            e_ref[rows, :] = e
            part = jnp.sum(e, axis=0, keepdims=True)
            total = part if total is None else total + part
        inverse = 1.0 / total
        out = None
        for b in range(count):
            rows = slice(b * shard, (b + 1) * shard)
            low = (e_ref[rows, :] * inverse).astype(BF16)
            term = dot(vt_ref[:, rows], low, NN)
            out = term if out is None else out + term
            dv_ref[rows, :] += dot(low, grad, NN)
        delta = jnp.sum(grad.astype(F32).T * out, axis=0, keepdims=True)
        factor = inverse * SCALE
        grad_q = None
        for b, piece in enumerate(pieces):
            rows = slice(b * shard, (b + 1) * shard)
            gp = dot(piece[:, vcol], grad, NT)
            gs = ((gp - delta) * factor * e_ref[rows, :]).astype(BF16)
            term = dot(kt_ref[:, rows], gs, NN)
            grad_q = term if grad_q is None else grad_q + term
            dk_ref[rows, :] += dot(gs, q, NN)
        here = pl.ds(pl.multiple_of(m * HEAD_SIZE, HEAD_SIZE), HEAD_SIZE)
        att_ref[:, here] = out.T.astype(BF16)
        dq_ref[:, here] = grad_q.T.astype(BF16)

    for b, term in enumerate(terms):
        rows = slice(b * shard, (b + 1) * shard)
        term[:, :HEAD_SIZE] = dk_ref[rows, :].astype(BF16)
        term[:, HEAD_SIZE:] = dv_ref[rows, :].astype(BF16)


def weights_kernel(ht, hto, ct, cto, dq, dqo, att, atto, out_ref):
    width = dq.shape[1]
    out_ref[:, :width] = (dot(ht[...], dq[...], NN) + dot(hto[...], dqo[...], NN)).astype(BF16)
    term = dot(ct[...], att[...], NN) + dot(cto[...], atto[...], NN)
    out_ref[:, width : 2 * width] = (2.0 * term).astype(BF16)


def fill_kernel(ht, hto, dkv, dkvo, _, out_ref, term_ref, sem):
    begin = out_ref.shape[1] - dkv.shape[1]
    term_ref[...] = (dot(ht[...], dkv[...], NN) + dot(hto[...], dkvo[...], NN)).astype(BF16)
    copy = pltpu.make_async_copy(term_ref, out_ref.at[:, begin:], sem)
    copy.start()
    copy.wait()


def previous_kernel(place, where, att, atto, next_ref, s0, s1, s2, s3, out_ref):
    half = att.shape[1]
    depth = s0.shape[0]
    for i, shard in enumerate((s0, s1, s2, s3)):
        term = dot(att[...], shard[:, group_columns(where[1], 2 * half, half)], NT)
        term += dot(atto[...], shard[:, group_columns(1 - where[1], 2 * half, half)], NT)
        for p in range(depth // LANES):
            to = block(place, i * (depth // LANES) + p)
            part = term[:, p * LANES : (p + 1) * LANES]
            out_ref[:, to] = (next_ref[:, to].astype(F32) - 2.0 * part).astype(BF16)


def group_columns(group, begin, width):
    return pl.ds(pl.multiple_of(begin + group * width, width), width)


def current_kernel(
    place, where, dq, dqo, dkv, dkvo, x_ref, cot_ref, q0, q1, q2, q3, k0, k1, k2, k3, out_ref, gh_ref
):
    half = dq.shape[1]
    depth = q0.shape[0]
    for i, shard in enumerate((q0, q1, q2, q3)):
        term = dot(dq[...], shard[:, group_columns(where[1], 0, half)], NT)
        term += dot(dqo[...], shard[:, group_columns(1 - where[1], 0, half)], NT)
        for p in range(depth // LANES):
            to = block(place, i * (depth // LANES) + p)
            gh_ref[:, to] = term[:, p * LANES : (p + 1) * LANES]
    for i, shard in enumerate((k0, k1, k2, k3)):
        to = whole(place, i, depth)
        term = gh_ref[:, to]
        for group, part in ((where[1], dkv), (1 - where[1], dkvo)):
            for begin in (0, HEAD_SIZE):
                columns = group_columns(group, KEY_VALUE_HEADS * begin, HEAD_SIZE)
                term += dot(part[:, begin : begin + HEAD_SIZE], shard[:, columns], NT)
        gh_ref[:, to] = term
    normed, inv_rms = normalize(x_ref[...])
    grad_hidden = gh_ref[...]
    mean = jnp.mean(grad_hidden * normed, axis=-1, keepdims=True)
    grad_x = inv_rms * (grad_hidden - normed * mean)
    out_ref[...] = (cot_ref[...].astype(F32) + grad_x).astype(BF16)


def sum_kernel(norm, where, terms, kept_ref, sent_ref, total):
    total[...] = terms[0].astype(F32)

    @pl.loop(1, terms.shape[0])
    def _(i):
        total[...] += terms[i].astype(F32)

    own = kept_ref.shape[0]
    kept_ref[...] = total[pl.ds(pl.multiple_of(where[1] * own, own), own), :] * norm
    sent_ref[...] = total[pl.ds(pl.multiple_of((1 - where[1]) * own, own), own), :] * norm


def assemble_kernel(where, kept, came, out_ref):
    half = GROUP * HEAD_SIZE
    ends = 2 * half + 2 * KEY_VALUE_HEADS * HEAD_SIZE
    for side, rows in ((where[1], kept), (1 - where[1], came)):
        out_ref[:, group_columns(side, 0, half)] = rows[:, :half]
        out_ref[:, group_columns(side, ends, half)] = rows[:, half : 2 * half]
        for i in range(2):
            to = group_columns(side, 2 * half + i * KEY_VALUE_HEADS * HEAD_SIZE, HEAD_SIZE)
            begin = 2 * half + i * HEAD_SIZE
            out_ref[:, to] = rows[:, begin : begin + HEAD_SIZE]


def shards(x_cur, x_next, cot_cur, cot_next, w_q, w_kv, w_out):
    seq_count, shard, width = x_cur.shape
    x_cur, x_next, cot_cur, cot_next = (
        v.reshape(seq_count * shard, width) for v in (x_cur, x_next, cot_cur, cot_next)
    )
    q_width, kv_width, depth = w_q.shape[1], w_kv.shape[1], w_q.shape[0]
    x, z, low, high, core = (lax.axis_index(a) for a in ("x", "z", "yl", "yh", "c"))
    ctx = lax.axis_index(CTX)
    token_total = seq_count * shard * lax.axis_size(CTX) * lax.axis_size(FSDP)
    colour = (x + 2 * z) % 4
    mine = 2 * high + core
    apart = 2 * (1 - high) + core
    per = depth // LANES
    place = jnp.stack(
        [mine * per + i for i in range(per)]
        + [(mine ^ 1) * per + i for i in range(per)]
        + [apart * per + (colour + i) % 4 for i in QUARTERS]
        + [(apart ^ 1) * per + (colour + i) % 4 for i in QUARTERS]
        + [mine, mine ^ 1, apart, apart ^ 1]
    ).astype(jnp.int32)

    kv_shards = gather_kv(w_kv)
    qo_shards = gather_qo(w_q, w_out, colour)

    rows = array((shard, width), BF16)
    turned = array((width, shard), BF16)
    hidden, hidden_placed, cot_placed, hidden_t, cot_t = call(
        prepare_kernel, [rows] * 3 + [turned] * 2, 1, [place, x_cur, cot_next], 8 * shard * width
    )
    (kv,) = call(
        kv_kernel,
        [array((shard, kv_width), BF16)],
        1,
        [place, hidden, *kv_shards],
        2 * shard * width * kv_width,
    )
    behind2 = shift(kv, 1)
    behind4 = shift(behind2, 1)
    behind2, crossing = lax.optimization_barrier((behind2, jnp.where(low == 0, kv, behind2)))
    behind1 = swap_low(crossing)
    crossing = jnp.where(low == 0, behind2, behind4)
    behind3 = swap_low(crossing)

    queries, grad_attn = call(
        query_kernel,
        [array((shard, q_width), BF16)] * 2,
        0,
        [hidden_placed, cot_placed, *qo_shards],
        4 * shard * width * q_width,
    )
    hidden_to = swap_cores(hidden_t)
    cot_to = swap_cores(cot_t)

    keys = shard + WINDOW_TOKENS
    half_q, half_kv = q_width // 2, kv_width // 2
    where = jnp.stack([ctx, core]).astype(jnp.int32)
    windows = [behind4, behind3, behind2, behind1, kv]

    def attend(which):
        att, dq, *terms = call(
            attention_kernel,
            [array((shard, half_q), BF16)] * 2 + [array((shard, half_kv), BF16)] * 5,
            1,
            [jnp.stack([ctx, which]).astype(jnp.int32), queries, grad_attn, *windows],
            6 * shard * keys * q_width,
            [
                pltpu.VMEM((HEAD_SIZE, keys), BF16),
                pltpu.VMEM((HEAD_SIZE, keys), BF16),
                pltpu.VMEM((keys, shard), F32),
                pltpu.VMEM((keys, HEAD_SIZE), F32),
                pltpu.VMEM((keys, HEAD_SIZE), F32),
            ],
        )
        return att, dq, terms

    def cross(terms):
        _, t3, _, t1, _ = terms
        third = swap_low(t3)
        first = swap_low(t1)
        return third, first

    def gather_terms(terms, crossed):
        t4, _, t2, _, t0, third, first = (v.astype(F32) for v in (*terms, *crossed))
        two_back = (t4 + jnp.where(low == 0, 0.0, third)).astype(BF16)
        two_back = shift(two_back, -1)
        one_back = t2 + jnp.where(low == 0, third, first) + two_back.astype(F32)
        one_back = one_back.astype(BF16)
        one_back = shift(one_back, -1)
        grad_kv = t0 + jnp.where(low == 0, first, 0.0) + one_back.astype(F32)
        return grad_kv.astype(BF16)

    att_sent, dq_sent, terms_sent = attend(1 - core)
    dq_came = swap_cores(dq_sent)
    att_came = swap_cores(att_sent)
    crossed = cross(terms_sent)
    att_kept, dq_kept, terms_kept = attend(core)
    dkv_sent = gather_terms(terms_sent, crossed)
    dkv_kept = gather_terms(terms_kept, cross(terms_kept))
    dkv_came = swap_cores(dkv_sent)

    chips = lax.axis_size(CHIPS)
    columns = q_width + half_kv
    (terms,) = call(
        weights_kernel,
        [array((width, columns), BF16)],
        0,
        [hidden_t, hidden_to, cot_t, cot_to, dq_kept, dq_came, att_kept, att_came],
        4 * shard * width * q_width,
    )
    turned_flops = 4 * shard * width * half_kv
    terms = pl.pallas_call(
        fill_kernel,
        name="fill_kernel",
        out_shape=array((width, columns), BF16),
        in_specs=[VMEM] * 4 + [pl.BlockSpec(memory_space=pl.ANY)],
        out_specs=pl.BlockSpec(memory_space=pl.ANY),
        scratch_shapes=[pltpu.VMEM((width, half_kv), BF16), pltpu.SemaphoreType.DMA(())],
        input_output_aliases={4: 0},
        cost_estimate=pl.CostEstimate(
            flops=turned_flops, bytes_accessed=4 * width * shard, transcendentals=0
        ),
        compiler_params=pltpu.CompilerParams(vmem_limit_bytes=16 * 2**20),
    )(hidden_t, hidden_to, dkv_kept, dkv_came, terms)
    terms = lax.all_to_all(terms.reshape(chips, width // chips, columns), CHIPS, 0, 0)

    (x_prev,) = call(
        previous_kernel,
        [rows],
        2,
        [place, where, att_kept, att_sent, x_next, *qo_shards],
        2 * shard * width * q_width,
    )
    (grad_cur,) = call(
        current_kernel,
        [rows],
        2,
        [place, where, dq_kept, dq_sent, dkv_kept, dkv_sent, x_cur, cot_cur]
        + [*qo_shards, *kv_shards],
        2 * shard * width * (q_width + kv_width),
        [pltpu.VMEM((shard, width), F32)],
    )

    own = width // chips // 2
    part = array((own, columns), F32)
    kept, sent = call(
        lambda *refs: sum_kernel(1.0 / math.sqrt(token_total), *refs),
        [part] * 2,
        1,
        [where, terms],
        width * columns,
        [pltpu.VMEM((2 * own, columns), F32)],
    )
    came = swap_cores(sent)
    (grad_weights,) = call(
        assemble_kernel, [array((own, 2 * columns), F32)], 1, [where, kept, came], own * columns
    )
    full = (seq_count, shard, width)
    return (x_prev.reshape(full), grad_cur.reshape(full), grad_weights)


def solution(mesh):
    mesh = Mesh(mesh.devices.reshape(4, 4, 2, 2, 2), CTX + FSDP)
    in_specs = (P(FSDP, CTX, None),) * 4 + (P(FSDP, None),) * 3
    out_specs = (P(FSDP, CTX, None), P(FSDP, CTX, None), P(CTX + FSDP, None))
    return jax.shard_map(shards, mesh=mesh, in_specs=in_specs, out_specs=out_specs, check_vma=False)
```

time: 946 us -> 253 us (0.27)
  the two profiles are of different devices: /device:TPU:0 before, /device:TPU:71 now
where the time goes in v2:
time: 253 us
  waiting for transfers between devices  115 us (45%)
  starting transfers between devices  64.5 us (25%)
  Pallas kernels  53.8 us (21%)
  local copies, waits for them, and re-layouts  16.7 us (7%)
    all_to_all x1, waiting for transfers between devices, shards(): lax.all_to_all(terms.reshape(chips, width // chips, columns), CHIPS, 0, 0)  61.7 us
    pallas_call x10, Pallas kernels, call(): pl.pallas_call(kernel, out_shape=outs, in_specs=[SMEM] * n_scalar + [VMEM...  51.5 us
    ppermute x6, starting transfers between devices, shift(): return lax.ppermute(value, ('x', 'z'), pairs)  24.8 us
    ppermute x2, waiting for transfers between devices, fetch(): return lax.ppermute(value, ('yl', 'yh'), [(0, 3), (3, 0), (1, 2), (2, 1)])  23.5 us
    ppermute x10, starting transfers between devices, swap_cores(): return lax.ppermute(value, 'c', [(0, 1), (1, 0)])  14.8 us
    unnamed x50, local copies, waits for them, and re-layouts  14.5 us
    all_to_all x1, starting transfers between devices, shards(): lax.all_to_all(terms.reshape(chips, width // chips, columns), CHIPS, 0, 0)  14 us
    ppermute x6, waiting for transfers between devices, shift(): return lax.ppermute(value, ('x', 'z'), pairs)  12.1 us
  transfers between devices with their start and end apart: 28, of which 12 were waited for; matrix products, arithmetic and copies ran while one was open for 2% of the time, Pallas kernels for 18%

profile of v2, /device:TPU:71, one launch (start us, length us, event | category | flops | bytes accessed | tf_op | source)
XLA Modules:
  0.0 252.7 jit_solution(4198355215355992159)
XLA Ops:
  0.7 1.2 constant_dynamic-slice_fusion
  1.9 2.8 %collective-permute-start.1 = (bf16[128,2048]{1,0:T(8,128)(2,1)S(1)}, bf16[128,2048]{1,0:T(8,128)(2,1)S(1)}, u32[]{:S(2)}, u32[]{:S(2)}) collective-permute-start(bf16[128,2048]{1,0:T(8,128)(2,1)S(1)} %pad_maximum_fusion), channel_id=1, source_target_pairs={{0,6},{6,0},{2,4},{4,2},{1,7},{7,1},{3,5},{5,3},{8,14},{14,8},{10,... | collective-permute-start | bytes 1572872 | tf_op jit(solution)/shard_map/ppermute | solution.py:78
  4.7 11.4 %collective-permute-done.1 = bf16[128,2048]{1,0:T(8,128)(2,1)S(1)} collective-permute-done((bf16[128,2048]{1,0:T(8,128)(2,1)S(1)}, bf16[128,2048]{1,0:T(8,128)(2,1)S(1)}, u32[]{:S(2)}, u32[]{:S(2)}) %collective-permute-start.1) | collective-permute-done | bytes 524320 | tf_op jit(solution)/shard_map/ppermute | solution.py:78
  16.4 1.3 collective-permute-start.3
  17.9 2.1 collective-permute-start
  20.9 7.3 %collective-permute-done.2 = bf16[128,2048]{1,0:T(8,128)(2,1)S(1)} collective-permute-done((bf16[128,2048]{1,0:T(8,128)(2,1)S(1)}, bf16[128,2048]{1,0:T(8,128)(2,1)S(1)}, u32[]{:S(2)}, u32[]{:S(2)}) %collective-permute-start.2) | collective-permute-done | bytes 524320 | tf_op jit(solution)/shard_map/ppermute | solution.py:68
  30.3 3.1 %collective-permute-done.4 = bf16[128,2048]{1,0:T(8,128)(2,1)S(1)} collective-permute-done((bf16[128,2048]{1,0:T(8,128)(2,1)S(1)}, bf16[128,2048]{1,0:T(8,128)(2,1)S(1)}, u32[]{:S(2)}, u32[]{:S(2)}) %collective-permute-start.4) | collective-permute-done | bytes 524320 | tf_op jit(solution)/shard_map/ppermute | solution.py:68
  34.2 0.9 collective-permute-start.5
  35.2 2.7 %collective-permute-start.7 = (bf16[512,512]{1,0:T(8,128)(2,1)}, bf16[512,512]{1,0:T(8,128)(2,1)}, u32[]{:S(2)}, u32[]{:S(2)}) collective-permute-start(bf16[512,512]{1,0:T(8,128)(2,1)} %k0.1), channel_id=1, source_target_pairs={{0,6},{6,0},{2,4},{4,2},{1,7},{7,1},{3,5},{5,3},{8,14},{14,8},{10,... | collective-permute-start | bytes 1572872 | tf_op jit(solution)/shard_map/ppermute | solution.py:78
  38.1 12.1 %collective-permute-done.7.s2.k2 = bf16[512,512]{1,0:T(8,128)(2,1)} collective-permute-done((bf16[512,512]{1,0:T(8,128)(2,1)}, bf16[512,512]{1,0:T(8,128)(2,1)}, u32[]{:S(2)}, u32[]{:S(2)}) %collective-permute-start.7) | collective-permute-done | bytes 524320 | tf_op jit(solution)/shard_map/ppermute | solution.py:78
  51.2 1.2 copy-done.11
  52.4 3.0 %shard_map.94 = (bf16[256,2048]{1,0:T(8,128)(2,1)S(1)}, bf16[256,2048]{1,0:T(8,128)(2,1)S(1)}, bf16[256,2048]{1,0:T(8,128)(2,1)S(1)}, bf16[2048,256]{1,0:T(8,128)(2,1)}, bf16[2048,256]{1,0:T(8,128)(2,1)S(1)}) custom-call(s32[20]{0:T(128)S(1)} %stack.102.place, bf16[256,2048]{1,0:T(8,128)(2,1)S(1)} %bitcast.31, bf16[256,2048]{1,0:T(8,128)(2,1)S(1)} %bitcast.34), custom_call_target="tpu_custom_call" | custom-call | flops 4194304 | bytes 7340112 | tf_op jit(solution)/shard_map/pallas_call | solution.py:35
  55.4 1.0 copy-done.3
  56.4 1.0 copy-done.5
  57.4 1.0 copy-done.7
  58.4 2.2 shard_map.96.k0
  60.6 4.4 %collective-permute-start.9 = (bf16[256,512]{1,0:T(8,128)(2,1)S(1)}, bf16[256,512]{1,0:T(8,128)(2,1)}, u32[]{:S(2)}, u32[]{:S(2)}) collective-permute-start(bf16[256,512]{1,0:T(8,128)(2,1)S(1)} %shard_map.96.k0), channel_id=1, source_target_pairs={{0,8},{8,16},{16,24},{24,32},{32,40},{40,48},{48,56},{56,64},{64,7... | collective-permute-start | bytes 786440 | tf_op jit(solution)/shard_map/ppermute | solution.py:74
  65.6 5.1 %collective-permute-done.9.k2 = bf16[256,512]{1,0:T(8,128)(2,1)} collective-permute-done((bf16[256,512]{1,0:T(8,128)(2,1)S(1)}, bf16[256,512]{1,0:T(8,128)(2,1)}, u32[]{:S(2)}, u32[]{:S(2)}) %collective-permute-start.9) | collective-permute-done | bytes 262176 | tf_op jit(solution)/shard_map/ppermute | solution.py:74
  70.6 4.2 %collective-permute-start.10 = (bf16[256,512]{1,0:T(8,128)(2,1)}, bf16[256,512]{1,0:T(8,128)(2,1)}, u32[]{:S(2)}, u32[]{:S(2)}) collective-permute-start(bf16[256,512]{1,0:T(8,128)(2,1)} %collective-permute-done.9.k2), channel_id=1, source_target_pairs={{0,8},{8,16},{16,24},{24,32},{32,40},{40,48},{48,56},{56,64},{64,7... | collective-permute-start | bytes 786440 | tf_op jit(solution)/shard_map/ppermute | solution.py:74
  75.0 4.8 %collective-permute-done.10.k4 = bf16[256,512]{1,0:T(8,128)(2,1)} collective-permute-done((bf16[256,512]{1,0:T(8,128)(2,1)}, bf16[256,512]{1,0:T(8,128)(2,1)}, u32[]{:S(2)}, u32[]{:S(2)}) %collective-permute-start.10) | collective-permute-done | bytes 262176 | tf_op jit(solution)/shard_map/ppermute | solution.py:74
  79.8 1.0 broadcast_select_fusion
  81.0 1.9 collective-permute-start.23
  82.8 1.2 copy-done.8
  84.1 5.2 %shard_map.95 = (bf16[256,1024]{1,0:T(8,128)(2,1)S(1)}, bf16[256,1024]{1,0:T(8,128)(2,1)S(1)}) custom-call(bf16[256,2048]{1,0:T(8,128)(2,1)S(1)} %copy-done.6, bf16[256,2048]{1,0:T(8,128)(2,1)S(1)} %copy-done.8, bf16[512,2048]{1,0:T(8,128)(2,1)S(1)} %constant_dynamic-update-slice_fusion.s0.q0, bf16[512,2048]{1,0:T(8,128)(2,1)} %collective-permute-done.s1.q1, ...), custom_call_target="tpu_custom_call" | custom-call | flops 2147483648 | bytes 11534336 | tf_op jit(solution)/shard_map/pallas_call | solution.py:35
  90.2 9.5 %shard_map.97 = (bf16[256,512]{1,0:T(8,128)(2,1)S(1)}, bf16[256,512]{1,0:T(8,128)(2,1)S(1)}, bf16[256,256]{1,0:T(8,128)(2,1)S(1)}, bf16[256,256]{1,0:T(8,128)(2,...) custom-call(s32[2]{0:T(128)S(1)} %pad_add_fusion.where.refs_0_, ...), custom_call_target="tpu_custom_call" | custom-call | flops 2013265920 | bytes 3538952 | tf_op jit(solution)/shard_map/pallas_call | solution.py:35
  99.8 1.8 collective-permute-start.13
  101.9 9.5 %shard_map.98 = (bf16[256,512]{1,0:T(8,128)(2,1)S(1)}, bf16[256,512]{1,0:T(8,128)(2,1)S(1)}, bf16[256,256]{1,0:T(8,128)(2,1)S(1)}, bf16[256,256]{1,0:T(8,128)(2,...) custom-call(s32[2]{0:T(128)S(1)} %pad_add_fusion.1.where, ...), custom_call_target="tpu_custom_call" | custom-call | flops 2013265920 | bytes 3538952 | tf_op jit(solution)/shard_map/pallas_call | solution.py:35
  111.4 1.3 collective-permute-start.17
  113.0 6.0 %collective-permute-done.18 = bf16[256,256]{1,0:T(8,128)(2,1)S(1)} collective-permute-done((bf16[256,256]{1,0:T(8,128)(2,1)S(1)}, bf16[256,256]{1,0:T(8,128)(2,1)S(1)}, u32[]{:S(2)}, u32[]{:S(2)}) %collective-permute-start.18) | collective-permute-done | bytes 131104 | tf_op jit(solution)/shard_map/ppermute | solution.py:63
  119.0 3.3 %collective-permute-start.15 = (bf16[256,256]{1,0:T(8,128)(2,1)S(1)}, bf16[256,256]{1,0:T(8,128)(2,1)S(1)}, u32[]{:S(2)}, u32[]{:S(2)}) collective-permute-start(bf16[256,256]{1,0:T(8,128)(2,1)S(1)} %fusion.7), channel_id=1, source_target_pairs={{8,0},{16,8},{24,16},{32,24},{40,32},{48,40},{56,48},{64,56},{72,6... | collective-permute-start | bytes 393224 | tf_op jit(solution)/shard_map/ppermute | solution.py:74
  122.3 2.0 collective-permute-start.24
  124.8 5.1 %collective-permute-start.19 = (bf16[256,256]{1,0:T(8,128)(2,1)S(1)}, bf16[256,256]{1,0:T(8,128)(2,1)S(1)}, u32[]{:S(2)}, u32[]{:S(2)}) collective-permute-start(bf16[256,256]{1,0:T(8,128)(2,1)S(1)} %fusion.15), channel_id=1, source_target_pairs={{8,0},{16,8},{24,16},{32,24},{40,32},{48,40},{56,48},{64,56},{72,6... | collective-permute-start | bytes 393224 | tf_op jit(solution)/shard_map/ppermute | solution.py:74
  130.0 1.8 collective-permute-done.19
  131.9 3.8 %collective-permute-start.16 = (bf16[256,256]{1,0:T(8,128)(2,1)S(1)}, bf16[256,256]{1,0:T(8,128)(2,1)S(1)}, u32[]{:S(2)}, u32[]{:S(2)}) collective-permute-start(bf16[256,256]{1,0:T(8,128)(2,1)S(1)} %fusion.5), channel_id=1, source_target_pairs={{8,0},{16,8},{24,16},{32,24},{40,32},{48,40},{56,48},{64,56},{72,6... | collective-permute-start | bytes 393224 | tf_op jit(solution)/shard_map/ppermute | solution.py:74
  135.7 4.0 %collective-permute-start.20 = (bf16[256,256]{1,0:T(8,128)(2,1)S(1)}, bf16[256,256]{1,0:T(8,128)(2,1)S(1)}, u32[]{:S(2)}, u32[]{:S(2)}) collective-permute-start(bf16[256,256]{1,0:T(8,128)(2,1)S(1)} %fusion.13), channel_id=1, source_target_pairs={{8,0},{16,8},{24,16},{32,24},{40,32},{48,40},{56,48},{64,56},{72,6... | collective-permute-start | bytes 393224 | tf_op jit(solution)/shard_map/ppermute | solution.py:74
  139.8 3.9 %shard_map.101._ = bf16[2048,1280]{1,0:T(8,128)(2,1)S(1)} custom-call(bf16[2048,256]{1,0:T(8,128)(2,1)} %get-tuple-element.49.ht, bf16[2048,256]{1,0:T(8,128)(2,1)} %collective-permute-done.21.hto, bf16[2048,256]{1,0:T(8,128)(2,1)S(1)} %copy-done.4, bf16[2048,256]{1,0:T(8,128)(2,1)S(1)} %collective-permute-done.23.cto, ...), custom_call_target="tpu_custom_call" | custom-call | flops 2147483648 | bytes 10485760 | tf_op jit(solution)/shard_map/pallas_call | solution.py:35
  143.8 4.0 %collective-permute-start.22 = (bf16[256,256]{1,0:T(8,128)(2,1)S(1)}, bf16[256,256]{1,0:T(8,128)(2,1)S(1)}, u32[]{:S(2)}, u32[]{:S(2)}) collective-permute-start(bf16[256,256]{1,0:T(8,128)(2,1)S(1)} %fusion.10.dkvo), channel_id=1, source_target_pairs={{0,1},{1,0},{2,3},{3,2},{4,5},{5,4},{6,7},{7,6},{8,9},{9,8},{10,11... | collective-permute-start | bytes 393224 | tf_op jit(solution)/shard_map/ppermute | solution.py:59
  148.8 2.3 fill_kernel.1
  151.2 2.4 copy-done
  153.6 14.0 %all-to-all-start = ((bf16[64,32,1280]{2,1,0:T(8,128)(2,1)}), bf16[64,32,1280]{2,1,0:T(8,128)(2,1)}, u32[]{:S(2)}, u32[]{:S(2)}) async-start(bf16[64,32,1280]{2,1,0:T(8,128)(2,1)} %bitcast.30), calls=%async_computation | async-start | bytes 10485760 | tf_op jit(solution)/shard_map/all_to_all | solution.py:431
  168.5 1.2 copy-done.14
  169.7 0.9 copy-done.20
  170.7 5.6 %shard_map.99 = bf16[256,2048]{1,0:T(8,128)(2,1)} custom-call(s32[20]{0:T(128)S(1)} %stack.102.place, s32[2]{0:T(128)S(1)} %pad_add_fusion.where.refs_0_, bf16[256,512]{1,0:T(8,128)(2,1)S(1)} %copy-done.10, bf16[256,512]{1,0:T(8,128)(2,1)S(1)} %copy-done.20, bf16[256,2048]{1,0:T(8,128)(2,1)S(1)} %bitcast.35, ...), custom_call_target="tpu_custom_call" | custom-call | flops 1073741824 | bytes 11010136 | tf_op jit(solution)/shard_map/pallas_call | solution.py:35
  176.3 61.7 %all-to-all-done.refs_1_ = bf16[64,32,1280]{2,1,0:T(8,128)(2,1)} async-done(((bf16[64,32,1280]{2,1,0:T(8,128)(2,1)}), bf16[64,32,1280]{2,1,0:T(8,128)(2,1)}, u32[]{:S(2)}, u32[]{:S(2)}) %all-to-all-start) | async-done | bytes 5242912 | tf_op jit(solution)/shard_map/all_to_all | solution.py:431
  238.0 3.7 %shard_map.102 = (f32[16,1280]{1,0:T(8,128)S(1)}, f32[16,1280]{1,0:T(8,128)S(1)}) custom-call(s32[2]{0:T(128)S(1)} %pad_add_fusion.where.refs_0_, bf16[64,32,1280]{2,1,0:T(8,128)(2,1)} %all-to-all-done.refs_1_), custom_call_target="tpu_custom_call" | custom-call | flops 2621440 | bytes 5406728 | tf_op jit(solution)/shard_map/pallas_call | solution.py:35
  241.6 2.2 collective-permute-start.26
  243.9 7.7 %shard_map.100 = bf16[256,2048]{1,0:T(8,128)(2,1)} custom-call(s32[20]{0:T(128)S(1)} %stack.102.place, s32[2]{0:T(128)S(1)} %pad_add_fusion.where.refs_0_, bf16[256,512]{1,0:T(8,128)(2,1)S(1)} %get-tuple-element.37.dq, bf16[256,512]{1,0:T(8,128)(2,1)S(1)} %copy-done.18, bf16[256,256]{1,0:T(8,128)(2,1)S(1)} %fusion.2.dkv, bf16[256,256]{1,0:T(8,128)(2,1)S(1)} %copy-done.16, ...), custom_call_target="tpu_custom_call" | custom-call | flops 1610612736 | bytes 14418008 | tf_op jit(solution)/shard_map/pallas_call | solution.py:35
  251.5 1.2 shard_map.103
  (84 shorter events, 10.6 us)
Async XLA Ops:
  0.6 15.7 %copy-start.21 = (bf16[512,1024]{1,0:T(8,128)(2,1)S(1)}, bf16[512,1024]{1,0:T(8,128)(2,1)}, u32[]{:S(2)}) copy-start(bf16[512,1024]{1,0:T(8,128)(2,1)} %param.11) | copy-start | bytes 3145732
  0.7 17.1 %copy-start.22 = (bf16[512,1024]{1,0:T(8,128)(2,1)S(1)}, bf16[512,1024]{1,0:T(8,128)(2,1)}, u32[]{:S(2)}) copy-start(bf16[512,1024]{1,0:T(8,128)(2,1)} %param.13) | copy-start | bytes 3145732
  1.9 14.2 %collective-permute-start.1 = (bf16[128,2048]{1,0:T(8,128)(2,1)S(1)}, bf16[128,2048]{1,0:T(8,128)(2,1)S(1)}, u32[]{:S(2)}, u32[]{:S(2)}) collective-permute-start(bf16[128,2048]{1,0:T(8,128)(2,1)S(1)} %pad_maximum_fusion), channel_id=1, source_target_pairs={{0,6},{6,0},{2,4},{4,2},{1,7},{7,1},{3,5},{5,3},{8,14},{14,8},{10,... | collective-permute-start | bytes 1572872 | tf_op jit(solution)/shard_map/ppermute | solution.py:78
  16.2 12.0 %collective-permute-start.2 = (bf16[128,2048]{1,0:T(8,128)(2,1)S(1)}, bf16[128,2048]{1,0:T(8,128)(2,1)S(1)}, u32[]{:S(2)}, u32[]{:S(2)}) collective-permute-start(bf16[128,2048]{1,0:T(8,128)(2,1)S(1)} %collective-permute-done.1), channel_id=1, source_target_pairs={{0,32},{32,64},{64,96},{96,0},{1,33},{33,65},{65,97},{97,1},{2,34}... | collective-permute-start | bytes 1572872 | tf_op jit(solution)/shard_map/ppermute | solution.py:68
  16.4 13.0 %collective-permute-start.3 = (bf16[128,2048]{1,0:T(8,128)(2,1)S(1)}, bf16[128,2048]{1,0:T(8,128)(2,1)S(1)}, u32[]{:S(2)}, u32[]{:S(2)}) collective-permute-start(bf16[128,2048]{1,0:T(8,128)(2,1)S(1)} %collective-permute-done.1), channel_id=1, source_target_pairs={{0,96},{32,0},{64,32},{96,64},{1,97},{33,1},{65,33},{97,65},{2,98}... | collective-permute-start | bytes 1572872 | tf_op jit(solution)/shard_map/ppermute | solution.py:68
  17.9 33.3 %copy-start.1 = (bf16[1,256,2048]{2,1,0:T(8,128)(2,1)S(1)}, bf16[1,256,2048]{2,1,0:T(8,128)(2,1)}, u32[]{:S(2)}) copy-start(bf16[1,256,2048]{2,1,0:T(8,128)(2,1)} %param.7) | copy-start | bytes 3145732
  17.9 63.1 %collective-permute-start = (bf16[512,2048]{1,0:T(8,128)(2,1)S(1)}, bf16[512,2048]{1,0:T(8,128)(2,1)}, u32[]{:S(2)}, u32[]{:S(2)}) collective-permute-start(bf16[512,2048]{1,0:T(8,128)(2,1)S(1)} %constant_dynamic-update-slice_fusion.s0.q0), channel_id=1, source_target_pairs={{0,1},{1,0},{2,3},{3,2},{4,5},{5,4},{6,7},{7,6},{8,9},{9,8},{10,11... | collective-permute-start | bytes 6291464 | tf_op jit(solution)/shard_map/ppermute | solution.py:59
  20.0 13.4 %collective-permute-start.4 = (bf16[128,2048]{1,0:T(8,128)(2,1)S(1)}, bf16[128,2048]{1,0:T(8,128)(2,1)S(1)}, u32[]{:S(2)}, u32[]{:S(2)}) collective-permute-start(bf16[128,2048]{1,0:T(8,128)(2,1)S(1)} %collective-permute-done.1), channel_id=1, source_target_pairs={{0,24},{8,0},{16,8},{24,16},{1,25},{9,1},{17,9},{25,17},{2,26},{10... | collective-permute-start | bytes 1572872 | tf_op jit(solution)/shard_map/ppermute | solution.py:68
  34.2 48.6 %collective-permute-start.5 = (bf16[512,2048]{1,0:T(8,128)(2,1)}, bf16[512,2048]{1,0:T(8,128)(2,1)}, u32[]{:S(2)}, u32[]{:S(2)}) collective-permute-start(bf16[512,2048]{1,0:T(8,128)(2,1)} %constant_dynamic-update-slice_fusion.2.s2.q2), channel_id=1, source_target_pairs={{0,1},{1,0},{2,3},{3,2},{4,5},{5,4},{6,7},{7,6},{8,9},{9,8},{10,11... | collective-permute-start | bytes 6291464 | tf_op jit(solution)/shard_map/ppermute | solution.py:59
  35.2 15.0 %collective-permute-start.7 = (bf16[512,512]{1,0:T(8,128)(2,1)}, bf16[512,512]{1,0:T(8,128)(2,1)}, u32[]{:S(2)}, u32[]{:S(2)}) collective-permute-start(bf16[512,512]{1,0:T(8,128)(2,1)} %k0.1), channel_id=1, source_target_pairs={{0,6},{6,0},{2,4},{4,2},{1,7},{7,1},{3,5},{5,3},{8,14},{14,8},{10,... | collective-permute-start | bytes 1572872 | tf_op jit(solution)/shard_map/ppermute | solution.py:78
  37.9 20.5 %collective-permute-start.6 = (bf16[512,512]{1,0:T(8,128)(2,1)}, bf16[512,512]{1,0:T(8,128)(2,1)}, u32[]{:S(2)}, u32[]{:S(2)}) collective-permute-start(bf16[512,512]{1,0:T(8,128)(2,1)} %k0.1), channel_id=1, source_target_pairs={{0,1},{1,0},{2,3},{3,2},{4,5},{5,4},{6,7},{7,6},{8,9},{9,8},{10,11... | collective-permute-start | bytes 1572872 | tf_op jit(solution)/shard_map/ppermute | solution.py:59
  50.2 8.2 %collective-permute-start.8 = (bf16[512,512]{1,0:T(8,128)(2,1)}, bf16[512,512]{1,0:T(8,128)(2,1)}, u32[]{:S(2)}, u32[]{:S(2)}) collective-permute-start(bf16[512,512]{1,0:T(8,128)(2,1)} %collective-permute-done.7.s2.k2), channel_id=1, source_target_pairs={{0,1},{1,0},{2,3},{3,2},{4,5},{5,4},{6,7},{7,6},{8,9},{9,8},{10,11... | collective-permute-start | bytes 1572872 | tf_op jit(solution)/shard_map/ppermute | solution.py:59
  51.2 1.2 copy-start.11
  55.4 1.0 copy-start.3
  56.4 1.0 copy-start.5
  57.4 1.0 copy-start.7
  60.6 28.6 %copy-start.12 = (bf16[256,512]{1,0:T(8,128)(2,1)}, bf16[256,512]{1,0:T(8,128)(2,1)S(1)}, u32[]{:S(2)}) copy-start(bf16[256,512]{1,0:T(8,128)(2,1)S(1)} %shard_map.96.k0) | copy-start | bytes 786436
  60.6 10.0 %collective-permute-start.9 = (bf16[256,512]{1,0:T(8,128)(2,1)S(1)}, bf16[256,512]{1,0:T(8,128)(2,1)}, u32[]{:S(2)}, u32[]{:S(2)}) collective-permute-start(bf16[256,512]{1,0:T(8,128)(2,1)S(1)} %shard_map.96.k0), channel_id=1, source_target_pairs={{0,8},{8,16},{16,24},{24,32},{32,40},{40,48},{48,56},{56,64},{64,7... | collective-permute-start | bytes 786440 | tf_op jit(solution)/shard_map/ppermute | solution.py:74
  65.1 70.7 %collective-permute-start.21 = (bf16[2048,256]{1,0:T(8,128)(2,1)}, bf16[2048,256]{1,0:T(8,128)(2,1)}, u32[]{:S(2)}, u32[]{:S(2)}) collective-permute-start(bf16[2048,256]{1,0:T(8,128)(2,1)} %get-tuple-element.49.ht), channel_id=1, source_target_pairs={{0,1},{1,0},{2,3},{3,2},{4,5},{5,4},{6,7},{7,6},{8,9},{9,8},{10,11... | collective-permute-start | bytes 3145736 | tf_op jit(solution)/shard_map/ppermute | solution.py:59
  70.6 9.2 %collective-permute-start.10 = (bf16[256,512]{1,0:T(8,128)(2,1)}, bf16[256,512]{1,0:T(8,128)(2,1)}, u32[]{:S(2)}, u32[]{:S(2)}) collective-permute-start(bf16[256,512]{1,0:T(8,128)(2,1)} %collective-permute-done.9.k2), channel_id=1, source_target_pairs={{0,8},{8,16},{16,24},{24,32},{32,40},{40,48},{48,56},{56,64},{64,7... | collective-permute-start | bytes 786440 | tf_op jit(solution)/shard_map/ppermute | solution.py:74
  74.9 7.9 %copy-start.6 = (bf16[256,2048]{1,0:T(8,128)(2,1)S(1)}, bf16[256,2048]{1,0:T(8,128)(2,1)}, u32[]{:S(2)}) copy-start(bf16[256,2048]{1,0:T(8,128)(2,1)} %copy-done.5) | copy-start | bytes 3145732
  74.9 14.3 %collective-permute-start.12 = (bf16[256,512]{1,0:T(8,128)(2,1)S(1)}, bf16[256,512]{1,0:T(8,128)(2,1)S(1)}, u32[]{:S(2)}, u32[]{:S(2)}) collective-permute-start(bf16[256,512]{1,0:T(8,128)(2,1)S(1)} %broadcast_select_fusion.1), channel_id=1, source_target_pairs={{0,4},{4,0},{1,5},{5,1},{2,6},{6,2},{3,7},{7,3},{8,12},{12,8},{9,1... | collective-permute-start | bytes 786440 | tf_op jit(solution)/shard_map/ppermute | solution.py:63
  80.8 8.5 %collective-permute-start.11 = (bf16[256,512]{1,0:T(8,128)(2,1)S(1)}, bf16[256,512]{1,0:T(8,128)(2,1)S(1)}, u32[]{:S(2)}, u32[]{:S(2)}) collective-permute-start(bf16[256,512]{1,0:T(8,128)(2,1)S(1)} %broadcast_select_fusion), channel_id=1, source_target_pairs={{0,4},{4,0},{1,5},{5,1},{2,6},{6,2},{3,7},{7,3},{8,12},{12,8},{9,1... | collective-permute-start | bytes 786440 | tf_op jit(solution)/shard_map/ppermute | solution.py:63
  81.0 58.8 %collective-permute-start.23 = (bf16[2048,256]{1,0:T(8,128)(2,1)}, bf16[2048,256]{1,0:T(8,128)(2,1)S(1)}, u32[]{:S(2)}, u32[]{:S(2)}) collective-permute-start(bf16[2048,256]{1,0:T(8,128)(2,1)} %copy-done.3), channel_id=1, source_target_pairs={{0,1},{1,0},{2,3},{3,2},{4,5},{5,4},{6,7},{7,6},{8,9},{9,8},{10,11... | collective-permute-start | bytes 3145736 | tf_op jit(solution)/shard_map/ppermute | solution.py:59
  82.8 1.2 copy-start.8
  99.8 40.1 %copy-start.9 = (bf16[256,512]{1,0:T(8,128)(2,1)}, bf16[256,512]{1,0:T(8,128)(2,1)S(1)}, u32[]{:S(2)}) copy-start(bf16[256,512]{1,0:T(8,128)(2,1)S(1)} %get-tuple-element.35.att) | copy-start | bytes 786436
  99.8 22.6 %collective-permute-start.13 = (bf16[256,256]{1,0:T(8,128)(2,1)S(1)}, bf16[256,256]{1,0:T(8,128)(2,1)S(1)}, u32[]{:S(2)}, u32[]{:S(2)}) collective-permute-start(bf16[256,256]{1,0:T(8,128)(2,1)S(1)} %get-tuple-element.40), channel_id=1, source_target_pairs={{0,4},{4,0},{1,5},{5,1},{2,6},{6,2},{3,7},{7,3},{8,12},{12,8},{9,1... | collective-permute-start | bytes 393224 | tf_op jit(solution)/shard_map/ppermute | solution.py:63
  101.6 11.1 %collective-permute-start.14 = (bf16[256,256]{1,0:T(8,128)(2,1)S(1)}, bf16[256,256]{1,0:T(8,128)(2,1)S(1)}, u32[]{:S(2)}, u32[]{:S(2)}) collective-permute-start(bf16[256,256]{1,0:T(8,128)(2,1)S(1)} %get-tuple-element.42), channel_id=1, source_target_pairs={{0,4},{4,0},{1,5},{5,1},{2,6},{6,2},{3,7},{7,3},{8,12},{12,8},{9,1... | collective-permute-start | bytes 393224 | tf_op jit(solution)/shard_map/ppermute | solution.py:63
  111.4 28.4 %copy-start.17 = (bf16[256,512]{1,0:T(8,128)(2,1)}, bf16[256,512]{1,0:T(8,128)(2,1)S(1)}, u32[]{:S(2)}) copy-start(bf16[256,512]{1,0:T(8,128)(2,1)S(1)} %get-tuple-element.38.dqo) | copy-start | bytes 786436
  111.4 28.4 %copy-start.19 = (bf16[256,512]{1,0:T(8,128)(2,1)}, bf16[256,512]{1,0:T(8,128)(2,1)S(1)}, u32[]{:S(2)}) copy-start(bf16[256,512]{1,0:T(8,128)(2,1)S(1)} %get-tuple-element.36.atto) | copy-start | bytes 786436
  111.4 28.4 %copy-start.4 = (bf16[2048,256]{1,0:T(8,128)(2,1)S(1)}, bf16[2048,256]{1,0:T(8,128)(2,1)}, u32[]{:S(2)}) copy-start(bf16[2048,256]{1,0:T(8,128)(2,1)} %copy-done.3) | copy-start | bytes 3145732
  111.4 12.9 %collective-permute-start.17 = (bf16[256,256]{1,0:T(8,128)(2,1)S(1)}, bf16[256,256]{1,0:T(8,128)(2,1)S(1)}, u32[]{:S(2)}, u32[]{:S(2)}) collective-permute-start(bf16[256,256]{1,0:T(8,128)(2,1)S(1)} %get-tuple-element.45), channel_id=1, source_target_pairs={{0,4},{4,0},{1,5},{5,1},{2,6},{6,2},{3,7},{7,3},{8,12},{12,8},{9,1... | collective-permute-start | bytes 393224 | tf_op jit(solution)/shard_map/ppermute | solution.py:63
  112.7 6.3 %collective-permute-start.18 = (bf16[256,256]{1,0:T(8,128)(2,1)S(1)}, bf16[256,256]{1,0:T(8,128)(2,1)S(1)}, u32[]{:S(2)}, u32[]{:S(2)}) collective-permute-start(bf16[256,256]{1,0:T(8,128)(2,1)S(1)} %get-tuple-element.47), channel_id=1, source_target_pairs={{0,4},{4,0},{1,5},{5,1},{2,6},{6,2},{3,7},{7,3},{8,12},{12,8},{9,1... | collective-permute-start | bytes 393224 | tf_op jit(solution)/shard_map/ppermute | solution.py:63
  119.0 5.8 %collective-permute-start.15 = (bf16[256,256]{1,0:T(8,128)(2,1)S(1)}, bf16[256,256]{1,0:T(8,128)(2,1)S(1)}, u32[]{:S(2)}, u32[]{:S(2)}) collective-permute-start(bf16[256,256]{1,0:T(8,128)(2,1)S(1)} %fusion.7), channel_id=1, source_target_pairs={{8,0},{16,8},{24,16},{32,24},{40,32},{48,40},{56,48},{64,56},{72,6... | collective-permute-start | bytes 393224 | tf_op jit(solution)/shard_map/ppermute | solution.py:74
  122.3 17.4 %collective-permute-start.24 = (bf16[256,512]{1,0:T(8,128)(2,1)S(1)}, bf16[256,512]{1,0:T(8,128)(2,1)S(1)}, u32[]{:S(2)}, u32[]{:S(2)}) collective-permute-start(bf16[256,512]{1,0:T(8,128)(2,1)S(1)} %get-tuple-element.38.dqo), channel_id=1, source_target_pairs={{0,1},{1,0},{2,3},{3,2},{4,5},{5,4},{6,7},{7,6},{8,9},{9,8},{10,11... | collective-permute-start | bytes 786440 | tf_op jit(solution)/shard_map/ppermute | solution.py:59
  124.3 15.5 %collective-permute-start.25 = (bf16[256,512]{1,0:T(8,128)(2,1)S(1)}, bf16[256,512]{1,0:T(8,128)(2,1)S(1)}, u32[]{:S(2)}, u32[]{:S(2)}) collective-permute-start(bf16[256,512]{1,0:T(8,128)(2,1)S(1)} %get-tuple-element.36.atto), channel_id=1, source_target_pairs={{0,1},{1,0},{2,3},{3,2},{4,5},{5,4},{6,7},{7,6},{8,9},{9,8},{10,11... | collective-permute-start | bytes 786440 | tf_op jit(solution)/shard_map/ppermute | solution.py:59
  124.8 7.1 %collective-permute-start.19 = (bf16[256,256]{1,0:T(8,128)(2,1)S(1)}, bf16[256,256]{1,0:T(8,128)(2,1)S(1)}, u32[]{:S(2)}, u32[]{:S(2)}) collective-permute-start(bf16[256,256]{1,0:T(8,128)(2,1)S(1)} %fusion.15), channel_id=1, source_target_pairs={{8,0},{16,8},{24,16},{32,24},{40,32},{48,40},{56,48},{64,56},{72,6... | collective-permute-start | bytes 393224 | tf_op jit(solution)/shard_map/ppermute | solution.py:74
  131.9 16.0 %collective-permute-start.16 = (bf16[256,256]{1,0:T(8,128)(2,1)S(1)}, bf16[256,256]{1,0:T(8,128)(2,1)S(1)}, u32[]{:S(2)}, u32[]{:S(2)}) collective-permute-start(bf16[256,256]{1,0:T(8,128)(2,1)S(1)} %fusion.5), channel_id=1, source_target_pairs={{8,0},{16,8},{24,16},{32,24},{40,32},{48,40},{56,48},{64,56},{72,6... | collective-permute-start | bytes 393224 | tf_op jit(solution)/shard_map/ppermute | solution.py:74
  135.7 8.0 %collective-permute-start.20 = (bf16[256,256]{1,0:T(8,128)(2,1)S(1)}, bf16[256,256]{1,0:T(8,128)(2,1)S(1)}, u32[]{:S(2)}, u32[]{:S(2)}) collective-permute-start(bf16[256,256]{1,0:T(8,128)(2,1)S(1)} %fusion.13), channel_id=1, source_target_pairs={{8,0},{16,8},{24,16},{32,24},{40,32},{48,40},{56,48},{64,56},{72,6... | collective-permute-start | bytes 393224 | tf_op jit(solution)/shard_map/ppermute | solution.py:74
  143.8 4.1 %copy-start.15 = (bf16[256,256]{1,0:T(8,128)(2,1)}, bf16[256,256]{1,0:T(8,128)(2,1)S(1)}, u32[]{:S(2)}) copy-start(bf16[256,256]{1,0:T(8,128)(2,1)S(1)} %fusion.10.dkvo) | copy-start | bytes 393220
  143.8 5.0 %collective-permute-start.22 = (bf16[256,256]{1,0:T(8,128)(2,1)S(1)}, bf16[256,256]{1,0:T(8,128)(2,1)S(1)}, u32[]{:S(2)}, u32[]{:S(2)}) collective-permute-start(bf16[256,256]{1,0:T(8,128)(2,1)S(1)} %fusion.10.dkvo), channel_id=1, source_target_pairs={{0,1},{1,0},{2,3},{3,2},{4,5},{5,4},{6,7},{7,6},{8,9},{9,8},{10,11... | collective-permute-start | bytes 393224 | tf_op jit(solution)/shard_map/ppermute | solution.py:59
  151.2 2.4 copy-start
  153.6 84.4 %all-to-all-start = ((bf16[64,32,1280]{2,1,0:T(8,128)(2,1)}), bf16[64,32,1280]{2,1,0:T(8,128)(2,1)}, u32[]{:S(2)}, u32[]{:S(2)}) async-start(bf16[64,32,1280]{2,1,0:T(8,128)(2,1)} %bitcast.30), calls=%async_computation | async-start | bytes 10485760 | tf_op jit(solution)/shard_map/all_to_all | solution.py:431
  168.5 1.2 copy-start.14
  238.0 5.9 %copy-start.2 = (bf16[1,256,2048]{2,1,0:T(8,128)(2,1)S(1)}, bf16[1,256,2048]{2,1,0:T(8,128)(2,1)}, u32[]{:S(2)}) copy-start(bf16[1,256,2048]{2,1,0:T(8,128)(2,1)} %param.9) | copy-start | bytes 3145732
  238.0 5.9 %copy-start.16 = (bf16[256,256]{1,0:T(8,128)(2,1)S(1)}, bf16[256,256]{1,0:T(8,128)(2,1)}, u32[]{:S(2)}) copy-start(bf16[256,256]{1,0:T(8,128)(2,1)} %copy-done.15) | copy-start | bytes 393220
  238.0 5.9 %copy-start.18 = (bf16[256,512]{1,0:T(8,128)(2,1)S(1)}, bf16[256,512]{1,0:T(8,128)(2,1)}, u32[]{:S(2)}) copy-start(bf16[256,512]{1,0:T(8,128)(2,1)} %copy-done.17) | copy-start | bytes 786436
  241.6 9.9 %collective-permute-start.26 = (f32[16,1280]{1,0:T(8,128)S(1)}, f32[16,1280]{1,0:T(8,128)S(1)}, u32[]{:S(2)}, u32[]{:S(2)}) collective-permute-start(f32[16,1280]{1,0:T(8,128)S(1)} %get-tuple-element.52), channel_id=1, source_target_pairs={{0,1},{1,0},{2,3},{3,2},{4,5},{5,4},{6,7},{7,6},{8,9},{9,8},{10,11... | collective-permute-start | bytes 245768 | tf_op jit(solution)/shard_map/ppermute | solution.py:59
  (3 other events, 2.9 us)
